TPU v7x, 128 devices: a whole 4x4x4 slice. The times are simulated.
128 devices in a mesh: dp: 16 (over x, y_hi, core), code: 8 (over y_lo, z).
Axes of the slice: x: 4, y: 4 (y_hi: 2, y_lo: 2; y = y_hi * 2 + y_lo), z: 4, core: 2. Of those that a mesh axis runs over, the one named last changes fastest.
Arguments:
- temporal_out: bfloat16 [2048, 4096], P('dp'), may hold values from -6 to 6
- depth_in: bfloat16 [8, 4096, 1024], P('code', 'dp'), may hold values from -0.09375 to 0.09375
- embed: bfloat16 [8, 1024, 1024], P('code'), may hold values from -6 to 6
- depth_w1: bfloat16 [8, 1024, 2112], P('code', None, 'dp'), may hold values from -0.1875 to 0.1875
- depth_w2: bfloat16 [8, 1024, 2112], P('code', None, 'dp'), may hold values from -0.125 to 0.125
- audio_tokens: int32 [2048, 8], P(None, 'code'), may hold values from 0 to 1023
- barge_mask: int32 [2048], P('dp'), may hold values 0 or 1
- out_grad: bfloat16 [2048, 8, 1024], P('dp', 'code'), may hold values from -6 to 6
Outputs:
- temporal_grad: bfloat16 [2048, 4096], P('dp', 'code')
- depth_in_grad: bfloat16 [8, 4096, 1024], P('code', 'dp')
- embed_grad: bfloat16 [8, 1024, 1024], P('code', 'dp')
- w1_grad: bfloat16 [8, 1024, 2112], P('code', None, 'dp')
- w2_grad: bfloat16 [8, 1024, 2112], P('code', None, 'dp')
All inputs are finite; a program needn't handle non-finite values. No bound on the sum of `barge_mask` on one device may be relied on, other than what follows from the above.
Results may differ from a plain program's by a relative error of at most 0.02.
Values may be sent and summed in bfloat16 or wider, within the bound.
No kernel may reach another device: no remote copies, remote signals or barrier semaphores. Data moves between devices by JAX's collectives and lax.ppermute only.
A program may use at most 128 MiB of HBM per device.

v0:
```python
import jax
import jax.numpy as jnp
from jax import lax
from jax.sharding import PartitionSpec as P

EPS = 1e-06


def shifted(block, axis, distance):
    devices = range(lax.axis_size(axis))
    route = [(i - distance, i) for i in devices if i - distance in devices]
    return lax.ppermute(block, axis, route)


def matmul(left, right):
    return jnp.dot(left, right, preferred_element_type=jnp.float32)


def contract_rows(left, right):
    return lax.dot_general(
        left, right, (((0,), (0,)), ((), ())), preferred_element_type=jnp.float32
    )


def contract_cols(left, right):
    return lax.dot_general(
        left, right, (((1,), (1,)), ((), ())), preferred_element_type=jnp.float32
    )


def silu_slope(values):
    sigma = jax.nn.sigmoid(values)
    return sigma * (1.0 + values * (1.0 - sigma))


def per_device(
    temporal_out, depth_in, embed, depth_w1, depth_w2, audio_tokens, barge_mask, out_grad
):
    dp_index = lax.axis_index("dp")
    n_code = lax.axis_size("code")
    own_rows = temporal_out.shape[0]
    projection = lax.all_gather(depth_in[0], "dp", axis=0, tiled=True)
    table = embed[0]
    token_all = audio_tokens[:, 0]
    token_own = lax.dynamic_slice_in_dim(token_all, dp_index * own_rows, own_rows, 0)
    depth_base = matmul(temporal_out, projection) + jnp.take(table, token_own, axis=0).astype(
        jnp.float32
    )
    width_depth = depth_base.shape[1]
    w_first, w_second = (
        lax.all_gather(depth_w1[0], "dp", axis=1, tiled=True),
        lax.all_gather(depth_w2[0], "dp", axis=1, tiled=True),
    )

    def depth_hidden(resid):
        scale = lax.rsqrt(jnp.mean(resid * resid, axis=-1, keepdims=True) + EPS)
        normed = (resid * scale).astype(jnp.bfloat16)
        pre_act = matmul(normed, w_first)
        active = jax.nn.silu(pre_act).astype(jnp.bfloat16)
        return (scale, normed, pre_act, active)

    def forward_turn(turn_index, incoming):
        resid = depth_base + incoming.astype(jnp.float32)
        scale, normed, pre_act, active = depth_hidden(resid)
        state = (resid + contract_cols(active, w_second)).astype(jnp.bfloat16)
        return shifted(state, "code", 1)

    start_state = jnp.zeros((own_rows, width_depth), jnp.bfloat16)
    incoming = lax.fori_loop(0, n_code - 1, forward_turn, start_state)
    resid = depth_base + incoming.astype(jnp.float32)
    scale, normed, pre_act, active = depth_hidden(resid)
    unit_rows = resid * scale
    derivative = silu_slope(pre_act)
    cotangent = out_grad[:, 0, :].astype(jnp.float32) * barge_mask.astype(jnp.float32)[:, None]

    def depth_back(from_next):
        state_slope = cotangent + from_next.astype(jnp.float32)
        slope_b = state_slope.astype(jnp.bfloat16)
        pre_slope = (matmul(slope_b, w_second) * derivative).astype(jnp.bfloat16)
        norm_slope = contract_cols(pre_slope, w_first)
        carried = (
            state_slope
            + scale
            * (norm_slope - unit_rows * jnp.mean(norm_slope * unit_rows, axis=-1, keepdims=True))
        ).astype(jnp.bfloat16)
        return (carried, slope_b, pre_slope)

    def backward_turn(turn_index, from_next):
        return shifted(depth_back(from_next)[0], "code", -1)

    from_next = lax.fori_loop(0, n_code - 1, backward_turn, start_state)
    carried, slope_b, pre_slope = depth_back(from_next)
    first_grad, second_grad = (
        lax.psum_scatter(
            contract_rows(normed, pre_slope).astype(jnp.bfloat16),
            "dp",
            scatter_dimension=1,
            tiled=True,
        ).astype(jnp.float32),
        lax.psum_scatter(
            contract_rows(slope_b, active).astype(jnp.bfloat16),
            "dp",
            scatter_dimension=1,
            tiled=True,
        ).astype(jnp.float32),
    )
    temporal_grad = lax.psum_scatter(
        contract_cols(carried, projection).astype(jnp.bfloat16),
        "code",
        scatter_dimension=1,
        tiled=True,
    )
    vocab_ids = lax.broadcasted_iota(jnp.int32, (1, table.shape[0]), 1)
    onehot = (token_own[:, None] == vocab_ids).astype(jnp.bfloat16)
    proj_grad, table_grad = (
        lax.psum_scatter(
            contract_rows(temporal_out, carried).astype(jnp.bfloat16),
            "dp",
            scatter_dimension=0,
            tiled=True,
        ).astype(jnp.float32),
        lax.psum_scatter(
            contract_rows(onehot, carried).astype(jnp.bfloat16),
            "dp",
            scatter_dimension=0,
            tiled=True,
        ).astype(jnp.float32),
    )
    return (
        temporal_grad,
        proj_grad.astype(jnp.bfloat16)[None],
        table_grad.astype(jnp.bfloat16)[None],
        first_grad.astype(jnp.bfloat16)[None],
        second_grad.astype(jnp.bfloat16)[None],
    )


def solution(mesh):
    in_specs = (
        P("dp", None),
        P("code", "dp", None),
        P("code", None, None),
        P("code", None, "dp"),
        P("code", None, "dp"),
        P(None, "code"),
        P("dp"),
        P("dp", "code", None),
    )
    out_specs = (
        P("dp", "code"),
        P("code", "dp", None),
        P("code", "dp", None),
        P("code", None, "dp"),
        P("code", None, "dp"),
    )
    return jax.shard_map(
        per_device, mesh=mesh, in_specs=in_specs, out_specs=out_specs, check_vma=False
    )
```

profile of v0, /device:TPU:1, one launch (start us, length us, event | category | flops | bytes accessed | tf_op | source)
XLA Modules:
  0.0 785.7 jit_solution(18314862474826231828)
XLA Ops:
  15.0 72.9 %all-gather.9.cloned.1.call-done = bf16[1,1024,2112]{1,0,2:T(2,128)(2,1)} async-done(((bf16[1,1024,132]{1,0,2:T(2,128)(2,1)}), bf16[1,1024,2112]{1,0,2:T(2,128)(2,1)}) %all-gather.9.cloned.1.call-update) | async-done | bytes 4325392 | tf_op jit(solution)/shard_map/all_gather | solution.py:51
  87.9 20.8 %copy.34 = bf16[1,1024,2112]{2,1,0:T(8,128)(2,1)} copy(bf16[1,1024,2112]{1,0,2:T(2,128)(2,1)} %all-gather.9.cloned.1.call-done) | data formatting | bytes 8650752
  108.7 53.2 %all-gather.11.cloned.1.call-done = bf16[1,1024,2112]{1,0,2:T(2,128)(2,1)} async-done(((bf16[1,1024,132]{1,0,2:T(2,128)(2,1)}), bf16[1,1024,2112]{1,0,2:T(2,128)(2,1)}) %all-gather.11.cloned.1.call-update) | async-done | bytes 4325392 | tf_op jit(solution)/shard_map/all_gather | solution.py:52
  161.9 20.9 %copy.35 = bf16[1,1024,2112]{2,1,0:T(8,128)(2,1)} copy(bf16[1,1024,2112]{1,0,2:T(2,128)(2,1)} %all-gather.11.cloned.1.call-done) | data formatting | bytes 8650752
  182.8 52.1 %all-gather.7.cloned.1.call-done = bf16[1,4096,1024]{2,1,0:T(8,128)(2,1)} async-done(((bf16[1,256,1024]{2,1,0:T(8,128)(2,1)}), bf16[1,4096,1024]{2,1,0:T(8,128)(2,1)}) %all-gather.7.cloned.1.call-update) | async-done | bytes 8388624 | tf_op jit(solution)/shard_map/all_gather | solution.py:42
  239.6 114.9 %while.20 = (s32[]{:T(128)}, bf16[128,1024]{1,0:T(8,128)(2,1)S(1)}, f32[128,1024]{1,0:T(8,128)S(1)}, bf16[1024,2112]{1,0:T(8,128)(2,1)}, bf16[1024,2112]{1,0:T(8,128)(2,1)}, /*index=5*/s32[]{:T(128)}) while((s32[]{:T(128)}, bf16[128,1024]{1,0:T(8,128)(2,1)S(1)}, f32[128,1024]{1,0:T(8,128)S(1)}, bf16[1024,2112]{1,0:T(8,128)(2,1)}, ...), condition=%wide.region_2.3_spmd, body=%wide.region_0.0_spmd.sunk | while | flops 1110220928 | bytes 11536493 | solution.py:69
  239.8 8.2 %fusion.71 = bf16[128,1024]{1,0:T(8,128)(2,1)S(1)} fusion(bf16[1024,2112]{1,0:T(8,128)(2,1)} %get-tuple-element.265, bf16[1024,2112]{1,0:T(8,128)(2,1)} %get-tuple-element.264, f32[128,1024]{1,0:T(8,128)S(1)} %get-tuple-element.263, bf16[128,1024]{1,0:T(8,128)(2,1)S(1)} %get-tuple-element.256, f32[128]{0:T(128)S(1)} %add_rsqrt_fusion.3), kind=kOutput, calls=%fused_computation.2.clone.1 | convolution fusion | flops 1109696512 | bytes 9699840 | tf_op jit(solution)/shard_map/while/body/eval_jaxpr/dot_general | solution.py:26
  256.7 8.2 %fusion.71 = bf16[128,1024]{1,0:T(8,128)(2,1)S(1)} fusion(bf16[1024,2112]{1,0:T(8,128)(2,1)} %get-tuple-element.265, bf16[1024,2112]{1,0:T(8,128)(2,1)} %get-tuple-element.264, f32[128,1024]{1,0:T(8,128)S(1)} %get-tuple-element.263, bf16[128,1024]{1,0:T(8,128)(2,1)S(1)} %get-tuple-element.256, f32[128]{0:T(128)S(1)} %add_rsqrt_fusion.3), kind=kOutput, calls=%fused_computation.2.clone.1 | convolution fusion | flops 1109696512 | bytes 9699840 | tf_op jit(solution)/shard_map/while/body/eval_jaxpr/dot_general | solution.py:26
  273.6 8.2 %fusion.71 = bf16[128,1024]{1,0:T(8,128)(2,1)S(1)} fusion(bf16[1024,2112]{1,0:T(8,128)(2,1)} %get-tuple-element.265, bf16[1024,2112]{1,0:T(8,128)(2,1)} %get-tuple-element.264, f32[128,1024]{1,0:T(8,128)S(1)} %get-tuple-element.263, bf16[128,1024]{1,0:T(8,128)(2,1)S(1)} %get-tuple-element.256, f32[128]{0:T(128)S(1)} %add_rsqrt_fusion.3), kind=kOutput, calls=%fused_computation.2.clone.1 | convolution fusion | flops 1109696512 | bytes 9699840 | tf_op jit(solution)/shard_map/while/body/eval_jaxpr/dot_general | solution.py:26
  289.7 8.2 %fusion.71 = bf16[128,1024]{1,0:T(8,128)(2,1)S(1)} fusion(bf16[1024,2112]{1,0:T(8,128)(2,1)} %get-tuple-element.265, bf16[1024,2112]{1,0:T(8,128)(2,1)} %get-tuple-element.264, f32[128,1024]{1,0:T(8,128)S(1)} %get-tuple-element.263, bf16[128,1024]{1,0:T(8,128)(2,1)S(1)} %get-tuple-element.256, f32[128]{0:T(128)S(1)} %add_rsqrt_fusion.3), kind=kOutput, calls=%fused_computation.2.clone.1 | convolution fusion | flops 1109696512 | bytes 9699840 | tf_op jit(solution)/shard_map/while/body/eval_jaxpr/dot_general | solution.py:26
  305.4 8.2 %fusion.71 = bf16[128,1024]{1,0:T(8,128)(2,1)S(1)} fusion(bf16[1024,2112]{1,0:T(8,128)(2,1)} %get-tuple-element.265, bf16[1024,2112]{1,0:T(8,128)(2,1)} %get-tuple-element.264, f32[128,1024]{1,0:T(8,128)S(1)} %get-tuple-element.263, bf16[128,1024]{1,0:T(8,128)(2,1)S(1)} %get-tuple-element.256, f32[128]{0:T(128)S(1)} %add_rsqrt_fusion.3), kind=kOutput, calls=%fused_computation.2.clone.1 | convolution fusion | flops 1109696512 | bytes 9699840 | tf_op jit(solution)/shard_map/while/body/eval_jaxpr/dot_general | solution.py:26
  320.8 8.2 %fusion.71 = bf16[128,1024]{1,0:T(8,128)(2,1)S(1)} fusion(bf16[1024,2112]{1,0:T(8,128)(2,1)} %get-tuple-element.265, bf16[1024,2112]{1,0:T(8,128)(2,1)} %get-tuple-element.264, f32[128,1024]{1,0:T(8,128)S(1)} %get-tuple-element.263, bf16[128,1024]{1,0:T(8,128)(2,1)S(1)} %get-tuple-element.256, f32[128]{0:T(128)S(1)} %add_rsqrt_fusion.3), kind=kOutput, calls=%fused_computation.2.clone.1 | convolution fusion | flops 1109696512 | bytes 9699840 | tf_op jit(solution)/shard_map/while/body/eval_jaxpr/dot_general | solution.py:26
  336.8 8.2 %fusion.71 = bf16[128,1024]{1,0:T(8,128)(2,1)S(1)} fusion(bf16[1024,2112]{1,0:T(8,128)(2,1)} %get-tuple-element.265, bf16[1024,2112]{1,0:T(8,128)(2,1)} %get-tuple-element.264, f32[128,1024]{1,0:T(8,128)S(1)} %get-tuple-element.263, bf16[128,1024]{1,0:T(8,128)(2,1)S(1)} %get-tuple-element.256, f32[128]{0:T(128)S(1)} %add_rsqrt_fusion.3), kind=kOutput, calls=%fused_computation.2.clone.1 | convolution fusion | flops 1109696512 | bytes 9699840 | tf_op jit(solution)/shard_map/while/body/eval_jaxpr/dot_general | solution.py:26
  360.8 125.3 %while.21 = (s32[]{:T(128)}, bf16[128,1024]{1,0:T(8,128)(2,1)S(1)}, f32[128,1024]{1,0:T(8,128)S(1)}, f32[128,1]{0,1:T(1,128)S(1)}, bf16[1024,2112]{1,0:T(8,128)(...) while((s32[]{:T(128)}, bf16[128,1024]{1,0:T(8,128)(2,1)S(1)}, ...), condition=%wide.region_6.7_spmd, body=%wide.region_4.6_spmd.sunk | while | flops 1109409792 | bytes 14715525 | solution.py:91
  360.8 8.2 %multiply_reduce_fusion.7 = (f32[128]{0:T(128)S(1)}, f32[128,1024]{1,0:T(8,128)S(1)}) fusion(f32[128,1024]{1,0:T(8,128)S(1)} %get-tuple-element.292, bf16[1024,2112]{1,0:T(8,128)(2,1)} %get-tuple-element.291, f32[128,2112]{0,1:T(8,128)S(1)} %get-tuple-element.290, bf16[1024,2112]{1,0:T(8,128)(2,1)} %get-tuple-element.289, ...), kind=kOutput, calls=%fused_computation.16.clone.1 | convolution fusion | flops 1108492160 | bytes 11567616 | tf_op jit(solution)/shard_map/while/body/eval_jaxpr/dot_general | solution.py:26
  370.6 8.4 %collective-permute-done.1 = bf16[128,1024]{1,0:T(8,128)(2,1)S(1)} collective-permute-done((bf16[128,1024]{1,0:T(8,128)(2,1)S(1)}, bf16[128,1024]{1,0:T(8,128)(2,1)S(1)}, u32[]{:S(2)}, u32[]{:S(2)}) %collective-permute-start.1) | collective-permute-done | bytes 262176 | tf_op jit(solution)/shard_map/while/body/eval_jaxpr/ppermute | solution.py:12
  378.9 8.2 %multiply_reduce_fusion.7 = (f32[128]{0:T(128)S(1)}, f32[128,1024]{1,0:T(8,128)S(1)}) fusion(f32[128,1024]{1,0:T(8,128)S(1)} %get-tuple-element.292, bf16[1024,2112]{1,0:T(8,128)(2,1)} %get-tuple-element.291, f32[128,2112]{0,1:T(8,128)S(1)} %get-tuple-element.290, bf16[1024,2112]{1,0:T(8,128)(2,1)} %get-tuple-element.289, ...), kind=kOutput, calls=%fused_computation.16.clone.1 | convolution fusion | flops 1108492160 | bytes 11567616 | tf_op jit(solution)/shard_map/while/body/eval_jaxpr/dot_general | solution.py:26
  388.7 8.4 %collective-permute-done.1 = bf16[128,1024]{1,0:T(8,128)(2,1)S(1)} collective-permute-done((bf16[128,1024]{1,0:T(8,128)(2,1)S(1)}, bf16[128,1024]{1,0:T(8,128)(2,1)S(1)}, u32[]{:S(2)}, u32[]{:S(2)}) %collective-permute-start.1) | collective-permute-done | bytes 262176 | tf_op jit(solution)/shard_map/while/body/eval_jaxpr/ppermute | solution.py:12
  397.0 8.2 %multiply_reduce_fusion.7 = (f32[128]{0:T(128)S(1)}, f32[128,1024]{1,0:T(8,128)S(1)}) fusion(f32[128,1024]{1,0:T(8,128)S(1)} %get-tuple-element.292, bf16[1024,2112]{1,0:T(8,128)(2,1)} %get-tuple-element.291, f32[128,2112]{0,1:T(8,128)S(1)} %get-tuple-element.290, bf16[1024,2112]{1,0:T(8,128)(2,1)} %get-tuple-element.289, ...), kind=kOutput, calls=%fused_computation.16.clone.1 | convolution fusion | flops 1108492160 | bytes 11567616 | tf_op jit(solution)/shard_map/while/body/eval_jaxpr/dot_general | solution.py:26
  406.8 8.4 %collective-permute-done.1 = bf16[128,1024]{1,0:T(8,128)(2,1)S(1)} collective-permute-done((bf16[128,1024]{1,0:T(8,128)(2,1)S(1)}, bf16[128,1024]{1,0:T(8,128)(2,1)S(1)}, u32[]{:S(2)}, u32[]{:S(2)}) %collective-permute-start.1) | collective-permute-done | bytes 262176 | tf_op jit(solution)/shard_map/while/body/eval_jaxpr/ppermute | solution.py:12
  415.1 8.2 %multiply_reduce_fusion.7 = (f32[128]{0:T(128)S(1)}, f32[128,1024]{1,0:T(8,128)S(1)}) fusion(f32[128,1024]{1,0:T(8,128)S(1)} %get-tuple-element.292, bf16[1024,2112]{1,0:T(8,128)(2,1)} %get-tuple-element.291, f32[128,2112]{0,1:T(8,128)S(1)} %get-tuple-element.290, bf16[1024,2112]{1,0:T(8,128)(2,1)} %get-tuple-element.289, ...), kind=kOutput, calls=%fused_computation.16.clone.1 | convolution fusion | flops 1108492160 | bytes 11567616 | tf_op jit(solution)/shard_map/while/body/eval_jaxpr/dot_general | solution.py:26
  424.8 8.4 %collective-permute-done.1 = bf16[128,1024]{1,0:T(8,128)(2,1)S(1)} collective-permute-done((bf16[128,1024]{1,0:T(8,128)(2,1)S(1)}, bf16[128,1024]{1,0:T(8,128)(2,1)S(1)}, u32[]{:S(2)}, u32[]{:S(2)}) %collective-permute-start.1) | collective-permute-done | bytes 262176 | tf_op jit(solution)/shard_map/while/body/eval_jaxpr/ppermute | solution.py:12
  433.2 8.2 %multiply_reduce_fusion.7 = (f32[128]{0:T(128)S(1)}, f32[128,1024]{1,0:T(8,128)S(1)}) fusion(f32[128,1024]{1,0:T(8,128)S(1)} %get-tuple-element.292, bf16[1024,2112]{1,0:T(8,128)(2,1)} %get-tuple-element.291, f32[128,2112]{0,1:T(8,128)S(1)} %get-tuple-element.290, bf16[1024,2112]{1,0:T(8,128)(2,1)} %get-tuple-element.289, ...), kind=kOutput, calls=%fused_computation.16.clone.1 | convolution fusion | flops 1108492160 | bytes 11567616 | tf_op jit(solution)/shard_map/while/body/eval_jaxpr/dot_general | solution.py:26
  442.9 7.9 %collective-permute-done.1 = bf16[128,1024]{1,0:T(8,128)(2,1)S(1)} collective-permute-done((bf16[128,1024]{1,0:T(8,128)(2,1)S(1)}, bf16[128,1024]{1,0:T(8,128)(2,1)S(1)}, u32[]{:S(2)}, u32[]{:S(2)}) %collective-permute-start.1) | collective-permute-done | bytes 262176 | tf_op jit(solution)/shard_map/while/body/eval_jaxpr/ppermute | solution.py:12
  450.9 8.2 %multiply_reduce_fusion.7 = (f32[128]{0:T(128)S(1)}, f32[128,1024]{1,0:T(8,128)S(1)}) fusion(f32[128,1024]{1,0:T(8,128)S(1)} %get-tuple-element.292, bf16[1024,2112]{1,0:T(8,128)(2,1)} %get-tuple-element.291, f32[128,2112]{0,1:T(8,128)S(1)} %get-tuple-element.290, bf16[1024,2112]{1,0:T(8,128)(2,1)} %get-tuple-element.289, ...), kind=kOutput, calls=%fused_computation.16.clone.1 | convolution fusion | flops 1108492160 | bytes 11567616 | tf_op jit(solution)/shard_map/while/body/eval_jaxpr/dot_general | solution.py:26
  460.6 7.9 %collective-permute-done.1 = bf16[128,1024]{1,0:T(8,128)(2,1)S(1)} collective-permute-done((bf16[128,1024]{1,0:T(8,128)(2,1)S(1)}, bf16[128,1024]{1,0:T(8,128)(2,1)S(1)}, u32[]{:S(2)}, u32[]{:S(2)}) %collective-permute-start.1) | collective-permute-done | bytes 262176 | tf_op jit(solution)/shard_map/while/body/eval_jaxpr/ppermute | solution.py:12
  468.5 8.2 %multiply_reduce_fusion.7 = (f32[128]{0:T(128)S(1)}, f32[128,1024]{1,0:T(8,128)S(1)}) fusion(f32[128,1024]{1,0:T(8,128)S(1)} %get-tuple-element.292, bf16[1024,2112]{1,0:T(8,128)(2,1)} %get-tuple-element.291, f32[128,2112]{0,1:T(8,128)S(1)} %get-tuple-element.290, bf16[1024,2112]{1,0:T(8,128)(2,1)} %get-tuple-element.289, ...), kind=kOutput, calls=%fused_computation.16.clone.1 | convolution fusion | flops 1108492160 | bytes 11567616 | tf_op jit(solution)/shard_map/while/body/eval_jaxpr/dot_general | solution.py:26
  478.2 7.9 %collective-permute-done.1 = bf16[128,1024]{1,0:T(8,128)(2,1)S(1)} collective-permute-done((bf16[128,1024]{1,0:T(8,128)(2,1)S(1)}, bf16[128,1024]{1,0:T(8,128)(2,1)S(1)}, u32[]{:S(2)}, u32[]{:S(2)}) %collective-permute-start.1) | collective-permute-done | bytes 262176 | tf_op jit(solution)/shard_map/while/body/eval_jaxpr/ppermute | solution.py:12
  502.8 7.2 fusion.17
  519.7 140.3 %fusion.49 = (bf16[1024,136]{0,1:T(8,128)(2,1)S(1)}, bf16[1024,136]{0,1:T(8,128)(2,1)S(1)}) fusion(bf16[1024,2112]{0,1:T(8,128)(2,1)} %convolution_convert_fusion.1, bf16[1024,2112]{0,1:T(8,128)(2,1)} %convolution_convert_fusion), kind=kCustom, calls=%all-reduce-scatter.2 | all-reduce-scatter fusion | flops 4456449 | bytes 9208320
  674.8 27.1 %reduce-scatter.8.cloned.1.call-done = bf16[128,512]{1,0:T(8,128)(2,1)} async-done(((bf16[128,4096]{1,0:T(8,128)(2,1)}), bf16[128,512]{1,0:T(8,128)(2,1)}) %reduce-scatter.8.cloned.1.call-update) | async-done | bytes 131088 | tf_op jit(solution)/shard_map/reduce_scatter | solution.py:107
  701.9 76.9 %reduce-scatter.12.cloned.1.call-done = bf16[64,1024]{1,0:T(8,128)(2,1)} async-done(((bf16[1024,1024]{1,0:T(8,128)(2,1)}), bf16[64,1024]{1,0:T(8,128)(2,1)}) %reduce-scatter.12.cloned.1.call-update) | async-done | bytes 131088 | tf_op jit(solution)/shard_map/reduce_scatter | solution.py:122
  (113 shorter events, 126.9 us)
Async XLA Ops:
  7.2 6.8 copy-start
  7.2 7.7 copy-start.4
  7.2 80.7 %all-gather.9.cloned.1.call-start = ((), (), s32[]{:S(2)}) async-start(), calls=%async_computation.7 | async-start | bytes 9191424 | tf_op jit(solution)/shard_map/all_gather | solution.py:51
  9.6 152.3 %all-gather.11.cloned.1.call-start = ((), (), s32[]{:S(2)}) async-start(), calls=%async_computation.8 | async-start | bytes 9191424 | tf_op jit(solution)/shard_map/all_gather | solution.py:52
  11.9 223.0 %all-gather.7.cloned.1.call-start = ((), (), s32[]{:S(2)}) async-start(), calls=%async_computation.6 | async-start | bytes 8912896 | tf_op jit(solution)/shard_map/all_gather | solution.py:42
  12.6 660.1 %reduce-scatter.10.cloned.1.call-start = ((), (), s32[]{:S(2)}) async-start(), calls=%async_computation.4 | async-start | bytes 8912896 | tf_op jit(solution)/shard_map/reduce_scatter | solution.py:116
  108.7 126.2 %copy-start.2 = (bf16[128,4096]{1,0:T(8,128)(2,1)S(1)}, bf16[128,4096]{1,0:T(8,128)(2,1)}, u32[]{:S(2)}) copy-start(bf16[128,4096]{1,0:T(8,128)(2,1)} %param.12) | copy-start | bytes 3145732
  247.9 8.6 %collective-permute-start = (bf16[128,1024]{1,0:T(8,128)(2,1)S(1)}, bf16[128,1024]{1,0:T(8,128)(2,1)S(1)}, u32[]{:S(2)}, u32[]{:S(2)}) collective-permute-start(bf16[128,1024]{1,0:T(8,128)(2,1)S(1)} %fusion.71), channel_id=1, source_target_pairs={{0,1},{1,2},{2,3},{3,4},{4,5},{5,6},{6,7},{8,9},{9,10},{10,11},{11... | collective-permute-start | bytes 786440 | tf_op jit(solution)/shard_map/while/body/eval_jaxpr/ppermute | solution.py:12
  264.9 8.6 %collective-permute-start = (bf16[128,1024]{1,0:T(8,128)(2,1)S(1)}, bf16[128,1024]{1,0:T(8,128)(2,1)S(1)}, u32[]{:S(2)}, u32[]{:S(2)}) collective-permute-start(bf16[128,1024]{1,0:T(8,128)(2,1)S(1)} %fusion.71), channel_id=1, source_target_pairs={{0,1},{1,2},{2,3},{3,4},{4,5},{5,6},{6,7},{8,9},{9,10},{10,11},{11... | collective-permute-start | bytes 786440 | tf_op jit(solution)/shard_map/while/body/eval_jaxpr/ppermute | solution.py:12
  281.8 7.7 collective-permute-start
  297.8 7.4 collective-permute-start
  313.6 7.1 collective-permute-start
  329.0 7.6 collective-permute-start
  344.9 9.5 %collective-permute-start = (bf16[128,1024]{1,0:T(8,128)(2,1)S(1)}, bf16[128,1024]{1,0:T(8,128)(2,1)S(1)}, u32[]{:S(2)}, u32[]{:S(2)}) collective-permute-start(bf16[128,1024]{1,0:T(8,128)(2,1)S(1)} %fusion.71), channel_id=1, source_target_pairs={{0,1},{1,2},{2,3},{3,4},{4,5},{5,6},{6,7},{8,9},{9,10},{10,11},{11... | collective-permute-start | bytes 786440 | tf_op jit(solution)/shard_map/while/body/eval_jaxpr/ppermute | solution.py:12
  360.8 125.3 %copy-start.5 = (bf16[128,1,1024]{2,0,1:T(8,128)(2,1)S(1)}, bf16[128,1,1024]{2,0,1:T(8,128)(2,1)}, u32[]{:S(2)}) copy-start(bf16[128,1,1024]{2,0,1:T(8,128)(2,1)} %param.19) | copy-start | bytes 786436
  369.3 9.7 %collective-permute-start.1 = (bf16[128,1024]{1,0:T(8,128)(2,1)S(1)}, bf16[128,1024]{1,0:T(8,128)(2,1)S(1)}, u32[]{:S(2)}, u32[]{:S(2)}) collective-permute-start(bf16[128,1024]{1,0:T(8,128)(2,1)S(1)} %add_convert_fusion.3), channel_id=1, source_target_pairs={{1,0},{2,1},{3,2},{4,3},{5,4},{6,5},{7,6},{9,8},{10,9},{11,10},{12... | collective-permute-start | bytes 786440 | tf_op jit(solution)/shard_map/while/body/eval_jaxpr/ppermute | solution.py:12
  387.4 9.7 %collective-permute-start.1 = (bf16[128,1024]{1,0:T(8,128)(2,1)S(1)}, bf16[128,1024]{1,0:T(8,128)(2,1)S(1)}, u32[]{:S(2)}, u32[]{:S(2)}) collective-permute-start(bf16[128,1024]{1,0:T(8,128)(2,1)S(1)} %add_convert_fusion.3), channel_id=1, source_target_pairs={{1,0},{2,1},{3,2},{4,3},{5,4},{6,5},{7,6},{9,8},{10,9},{11,10},{12... | collective-permute-start | bytes 786440 | tf_op jit(solution)/shard_map/while/body/eval_jaxpr/ppermute | solution.py:12
  405.5 9.7 %collective-permute-start.1 = (bf16[128,1024]{1,0:T(8,128)(2,1)S(1)}, bf16[128,1024]{1,0:T(8,128)(2,1)S(1)}, u32[]{:S(2)}, u32[]{:S(2)}) collective-permute-start(bf16[128,1024]{1,0:T(8,128)(2,1)S(1)} %add_convert_fusion.3), channel_id=1, source_target_pairs={{1,0},{2,1},{3,2},{4,3},{5,4},{6,5},{7,6},{9,8},{10,9},{11,10},{12... | collective-permute-start | bytes 786440 | tf_op jit(solution)/shard_map/while/body/eval_jaxpr/ppermute | solution.py:12
  423.5 9.7 %collective-permute-start.1 = (bf16[128,1024]{1,0:T(8,128)(2,1)S(1)}, bf16[128,1024]{1,0:T(8,128)(2,1)S(1)}, u32[]{:S(2)}, u32[]{:S(2)}) collective-permute-start(bf16[128,1024]{1,0:T(8,128)(2,1)S(1)} %add_convert_fusion.3), channel_id=1, source_target_pairs={{1,0},{2,1},{3,2},{4,3},{5,4},{6,5},{7,6},{9,8},{10,9},{11,10},{12... | collective-permute-start | bytes 786440 | tf_op jit(solution)/shard_map/while/body/eval_jaxpr/ppermute | solution.py:12
  441.6 9.2 %collective-permute-start.1 = (bf16[128,1024]{1,0:T(8,128)(2,1)S(1)}, bf16[128,1024]{1,0:T(8,128)(2,1)S(1)}, u32[]{:S(2)}, u32[]{:S(2)}) collective-permute-start(bf16[128,1024]{1,0:T(8,128)(2,1)S(1)} %add_convert_fusion.3), channel_id=1, source_target_pairs={{1,0},{2,1},{3,2},{4,3},{5,4},{6,5},{7,6},{9,8},{10,9},{11,10},{12... | collective-permute-start | bytes 786440 | tf_op jit(solution)/shard_map/while/body/eval_jaxpr/ppermute | solution.py:12
  459.3 9.2 %collective-permute-start.1 = (bf16[128,1024]{1,0:T(8,128)(2,1)S(1)}, bf16[128,1024]{1,0:T(8,128)(2,1)S(1)}, u32[]{:S(2)}, u32[]{:S(2)}) collective-permute-start(bf16[128,1024]{1,0:T(8,128)(2,1)S(1)} %add_convert_fusion.3), channel_id=1, source_target_pairs={{1,0},{2,1},{3,2},{4,3},{5,4},{6,5},{7,6},{9,8},{10,9},{11,10},{12... | collective-permute-start | bytes 786440 | tf_op jit(solution)/shard_map/while/body/eval_jaxpr/ppermute | solution.py:12
  476.9 9.2 %collective-permute-start.1 = (bf16[128,1024]{1,0:T(8,128)(2,1)S(1)}, bf16[128,1024]{1,0:T(8,128)(2,1)S(1)}, u32[]{:S(2)}, u32[]{:S(2)}) collective-permute-start(bf16[128,1024]{1,0:T(8,128)(2,1)S(1)} %add_convert_fusion.3), channel_id=1, source_target_pairs={{1,0},{2,1},{3,2},{4,3},{5,4},{6,5},{7,6},{9,8},{10,9},{11,10},{12... | collective-permute-start | bytes 786440 | tf_op jit(solution)/shard_map/while/body/eval_jaxpr/ppermute | solution.py:12
  491.6 5.6 copy-start.3
  502.8 199.1 %reduce-scatter.8.cloned.1.call-start = ((), (), s32[]{:S(2)}) async-start(), calls=%async_computation.3 | async-start | bytes 1179648 | tf_op jit(solution)/shard_map/reduce_scatter | solution.py:107
  510.1 268.7 %reduce-scatter.12.cloned.1.call-start = ((), (), s32[]{:S(2)}) async-start(), calls=%async_computation.5 | async-start | bytes 2228224 | tf_op jit(solution)/shard_map/reduce_scatter | solution.py:122
  513.0 3.3 copy-start.7
  519.7 148.2 %copy-start.6 = (u32[128]{0:T(128)S(1)}, u32[128]{0:T(128)}, u32[]{:S(2)}) copy-start(u32[128]{0:T(128)} %constant.72) | copy-start | bytes 1540
  519.7 259.1 %copy-start.1 = (bf16[1,1024,1024]{2,1,0:T(8,128)(2,1)S(1)}, bf16[1,1024,1024]{2,1,0:T(8,128)(2,1)}, u32[]{:S(2)}) copy-start(bf16[1,1024,1024]{2,1,0:T(8,128)(2,1)} %param.14) | copy-start | bytes 6291460
  660.1 9.1 %collective-permute-start.3 = (bf16[1024,60]{0,1:T(8,128)(2,1)S(1)}, bf16[1024,60]{0,1:T(8,128)(2,1)S(1)}, u32[]{:S(2)}, u32[]{:S(2)}) collective-permute-start(bf16[1024,60]{0,1:T(8,128)(2,1)S(1)} %slice.3), channel_id=1, source_target_pairs={{0,8},{8,16},{16,24},{24,32},{32,40},{40,48},{48,56},{56,64},{64,7... | collective-permute-start | bytes 368648
  666.0 3.9 collective-permute-start.2
Sparse Core Ops, SparseCore 0:
  10.4 77.3 all-gather.8
  90.3 71.6 all-gather.10
  164.3 70.5 all-gather.6
  502.9 160.7 reduce-scatter.9
  666.5 35.3 reduce-scatter.7
  706.3 72.5 reduce-scatter.11
where the time goes:
time: 789 us; the launch traced here: 786 us
  waiting for transfers between devices  367 us (47%)
  matrix products  158 us (20%)
  blocking collectives  140 us (18%)
  local copies, waits for them, and re-layouts  53.7 us (7%)
  starting transfers between devices  47 us (6%)
  between operations  15 us (2%)
    unnamed x1, blocking collectives  140 us
    dot_general x16, matrix products, contract_cols(): lax.dot_general(left, right, (((1,), (1,)), ((), ())), preferred_element_...  127 us
    ppermute x14, waiting for transfers between devices, shifted(): return lax.ppermute(block, axis, route)  83.9 us
    reduce_scatter x1, waiting for transfers between devices, per_device(): lax.psum_scatter(contract_rows(onehot, carried).astype(jnp.bfloat16), 'dp...  76.9 us
    all_gather x1, waiting for transfers between devices, per_device(): lax.all_gather(depth_w1[0], 'dp', axis=1, tiled=True)  72.9 us
    all_gather x1, waiting for transfers between devices, per_device(): lax.all_gather(depth_w2[0], 'dp', axis=1, tiled=True)  53.2 us
    all_gather x1, waiting for transfers between devices, per_device(): projection = lax.all_gather(depth_in[0], 'dp', axis=0, tiled=True)  52.1 us
    unnamed x26, local copies, waits for them, and re-layouts  50.6 us
  transfers between devices with their start and end apart: 22, of which 20 were waited for; matrix products, arithmetic and copies ran while one was open for 27% of the time, Pallas kernels for 0%

commit v1 on v0

v1 whole, which is shorter than its diff:
```python
import functools

import jax
import jax.numpy as jnp
from jax import lax
from jax.experimental import pallas as pl
from jax.experimental.pallas import tpu as pltpu
from jax.sharding import PartitionSpec as P

EPS = 1e-06
F32 = jnp.float32
BF16 = jnp.bfloat16
SUBLANES = 8


def dot_nn(left, right):
    return lax.dot_general(left, right, (((1,), (0,)), ((), ())), preferred_element_type=F32)


def dot_nt(left, right):
    return lax.dot_general(left, right, (((1,), (1,)), ((), ())), preferred_element_type=F32)


def shifted(block, axis, distance):
    devices = range(lax.axis_size(axis))
    route = [(i - distance, i) for i in devices if i - distance in devices]
    return lax.ppermute(block, axis, route)


VMEM = pl.BlockSpec(memory_space=pltpu.VMEM)


def params(megabytes):
    return pltpu.CompilerParams(vmem_limit_bytes=megabytes * 1024 * 1024)


def base_kernel(t_ref, w_ref, emb_ref, out_ref):
    step = pl.program_id(0)

    @pl.when(step == 0)
    def _():
        out_ref[...] = emb_ref[...].astype(F32)

    out_ref[...] += dot_nn(t_ref[...], w_ref[0])


def depth_base(temporal, gathered, token_rows, n_dp, piece):
    rows, _ = temporal.shape
    width = gathered.shape[-1]
    return pl.pallas_call(
        base_kernel,
        grid=(n_dp,),
        in_specs=[
            pl.BlockSpec((rows, piece), lambda s: (0, s)),
            pl.BlockSpec((1, piece, width), lambda s: (s, 0, 0)),
            pl.BlockSpec((rows, width), lambda s: (0, 0)),
        ],
        out_specs=pl.BlockSpec((rows, width), lambda s: (0, 0)),
        out_shape=jax.ShapeDtypeStruct((rows, width), F32),
        cost_estimate=pl.CostEstimate(
            flops=2 * rows * width * piece * n_dp,
            bytes_accessed=2 * width * piece * n_dp,
            transcendentals=0,
        ),
        name="depth_base",
    )(temporal, gathered, token_rows)


def chunk_sizes(hidden):
    size = hidden // 4 if hidden % (4 * SUBLANES) == 0 else hidden
    return [(start, size) for start in range(0, hidden, size)]


def normalise(resid):
    scale = lax.rsqrt(jnp.mean(resid * resid, axis=-1, keepdims=True) + EPS)
    return scale, (resid * scale).astype(BF16)


def forward_kernel(base_ref, in_ref, w1_ref, w2_ref, out_ref):
    resid = base_ref[...] + in_ref[...].astype(F32)
    _, normed = normalise(resid)
    total = resid
    for start, size in chunk_sizes(w1_ref.shape[0]):
        pre = dot_nt(normed, w1_ref[pl.ds(start, size), :])
        active = (pre * jax.nn.sigmoid(pre)).astype(BF16)
        total = total + dot_nn(active, w2_ref[pl.ds(start, size), :])
    out_ref[...] = total.astype(BF16)


def last_forward_kernel(
    base_ref, in_ref, w1_ref, unit_ref, scale_ref, normed_ref, slope_ref, active_ref
):
    resid = base_ref[...] + in_ref[...].astype(F32)
    scale, normed = normalise(resid)
    unit_ref[...] = resid * scale
    scale_ref[...] = scale
    normed_ref[...] = normed
    for start, size in chunk_sizes(w1_ref.shape[0]):
        pre = dot_nt(normed, w1_ref[pl.ds(start, size), :])
        sigma = jax.nn.sigmoid(pre)
        slope_ref[:, pl.ds(start, size)] = sigma * (1.0 + pre * (1.0 - sigma))
        active_ref[pl.ds(start, size), :] = (pre * sigma).astype(BF16).T


def backward_kernel(last, cot_ref, next_ref, w1_ref, w2_ref, unit_ref, scale_ref, slope_ref,
                    carry_ref, *saved):
    state_slope = cot_ref[...] + next_ref[...].astype(F32)
    slope_b = state_slope.astype(BF16)
    norm_slope = jnp.zeros(state_slope.shape, F32)
    for start, size in chunk_sizes(w1_ref.shape[0]):
        hidden = dot_nt(slope_b, w2_ref[pl.ds(start, size), :])
        pre_slope = (hidden * slope_ref[:, pl.ds(start, size)]).astype(BF16)
        if last:
            saved[1][pl.ds(start, size), :] = pre_slope.T
        norm_slope = norm_slope + dot_nn(pre_slope, w1_ref[pl.ds(start, size), :])
    unit = unit_ref[...]
    mean = jnp.mean(norm_slope * unit, axis=-1, keepdims=True)
    carry_ref[...] = (state_slope + scale_ref[...] * (norm_slope - unit * mean)).astype(BF16)
    if last:
        saved[0][...] = slope_b


def turn(kernel, operands, outs, rows, hidden, width, name, passes=2):
    return pl.pallas_call(
        kernel,
        in_specs=[VMEM] * len(operands),
        out_specs=jax.tree.map(lambda _: VMEM, outs),
        out_shape=outs,
        compiler_params=params(40),
        cost_estimate=pl.CostEstimate(
            flops=2 * passes * rows * hidden * width,
            bytes_accessed=2 * passes * hidden * width,
            transcendentals=0,
        ),
        name=name,
    )(*operands)


def term_kernel(c_ref, w_ref, out_ref):
    out_ref[0] = dot_nt(c_ref[...], w_ref[0]).astype(BF16)


def temporal_terms(carried, gathered, n_dp, n_code, piece):
    rows, width = carried.shape
    per = n_dp // n_code
    return pl.pallas_call(
        term_kernel,
        grid=(n_dp,),
        in_specs=[
            pl.BlockSpec((rows, width), lambda s: (0, 0)),
            pl.BlockSpec((1, piece, width), lambda s: (s, 0, 0)),
        ],
        out_specs=pl.BlockSpec((1, rows, piece), lambda s: (s // per, 0, s % per)),
        out_shape=jax.ShapeDtypeStruct((n_code, rows, piece * per), BF16),
        cost_estimate=pl.CostEstimate(
            flops=2 * rows * width * piece * n_dp,
            bytes_accessed=2 * width * piece * n_dp,
            transcendentals=0,
        ),
        name="temporal_terms",
    )(carried, gathered)


def grads_kernel(lc_ref, ls_ref, g_ref, oc_ref, os_ref, ac_ref, as_ref):
    step = pl.program_id(0)
    width = oc_ref.shape[1]

    @pl.when(step == 0)
    def _():
        ac_ref[...] = jnp.zeros_like(ac_ref)
        as_ref[...] = jnp.zeros_like(as_ref)

    ac_ref[...] += dot_nn(lc_ref[...], g_ref[:, :width])
    as_ref[...] += dot_nn(ls_ref[...], g_ref[:, width:])

    @pl.when(step == pl.num_programs(0) - 1)
    def _():
        oc_ref[...] = ac_ref[...].astype(BF16)
        os_ref[...] = as_ref[...].astype(BF16)


def final_grads(left_carry, left_slope, gathered):
    frames, both = gathered.shape
    width = both // 2
    block = 512 if frames % 512 == 0 else frames
    mc, ms = left_carry.shape[0], left_slope.shape[0]
    return pl.pallas_call(
        grads_kernel,
        grid=(frames // block,),
        in_specs=[
            pl.BlockSpec((mc, block), lambda s: (0, s)),
            pl.BlockSpec((ms, block), lambda s: (0, s)),
            pl.BlockSpec((block, both), lambda s: (s, 0)),
        ],
        out_specs=[
            pl.BlockSpec((mc, width), lambda s: (0, 0)),
            pl.BlockSpec((ms, width), lambda s: (0, 0)),
        ],
        out_shape=[
            jax.ShapeDtypeStruct((mc, width), BF16),
            jax.ShapeDtypeStruct((ms, width), BF16),
        ],
        scratch_shapes=[pltpu.VMEM((mc, width), F32), pltpu.VMEM((ms, width), F32)],
        cost_estimate=pl.CostEstimate(
            flops=2 * (mc + ms) * width * frames,
            bytes_accessed=2 * frames * both,
            transcendentals=0,
        ),
        name="final_grads",
    )(left_carry, left_slope, gathered)


def per_device(
    temporal_out, depth_in, embed, depth_w1, depth_w2, audio_tokens, barge_mask, out_grad
):
    dp_index = lax.axis_index("dp")
    n_dp, n_code = lax.axis_size("dp"), lax.axis_size("code")
    rows = temporal_out.shape[0]
    piece, width = depth_in.shape[1:]
    own_hidden = depth_w1.shape[2]
    table = embed[0]

    pad_hidden = -own_hidden % SUBLANES
    held = own_hidden + pad_hidden
    hidden = held * n_dp
    pad = ((0, pad_hidden), (0, 0))
    shard = jnp.concatenate(
        [depth_in[0], jnp.pad(depth_w1[0].T, pad), jnp.pad(depth_w2[0].T, pad)], axis=0
    )
    gathered = lax.all_gather(shard, "dp", axis=0)
    w_first = gathered[:, piece:piece + held].reshape(hidden, width)
    w_second = gathered[:, piece + held:].reshape(hidden, width)

    token_all = audio_tokens[:, 0]
    token_own = lax.dynamic_slice_in_dim(token_all, dp_index * rows, rows, 0)
    token_rows = jnp.take(table, token_own, axis=0)
    base = depth_base(temporal_out, gathered, token_rows, n_dp, piece)
    temporal_all = lax.all_gather(
        lax.optimization_barrier((temporal_out, base))[0], "dp", axis=0, tiled=True
    )

    state_type = jax.ShapeDtypeStruct((rows, width), BF16)
    incoming = jnp.zeros((rows, width), BF16)
    for _ in range(n_code - 1):
        state = turn(
            forward_kernel, (base, incoming, w_first, w_second), state_type,
            rows, hidden, width, "forward_turn",
        )
        incoming = shifted(state, "code", 1)
    unit, scale, normed, slope, active = turn(
        last_forward_kernel, (base, incoming, w_first),
        [
            jax.ShapeDtypeStruct((rows, width), F32),
            jax.ShapeDtypeStruct((rows, 1), F32),
            state_type,
            jax.ShapeDtypeStruct((rows, hidden), F32),
            jax.ShapeDtypeStruct((hidden, rows), BF16),
        ],
        rows, hidden, width, "last_forward_turn", passes=1,
    )
    normed_all = lax.all_gather(normed, "dp", axis=0, tiled=True)

    cotangent = out_grad[:, 0, :].astype(F32) * barge_mask.astype(F32)[:, None]
    from_next = jnp.zeros((rows, width), BF16)
    for step in range(n_code):
        last = step == n_code - 1
        outs = [state_type]
        if last:
            outs += [state_type, jax.ShapeDtypeStruct((hidden, rows), BF16)]
        results = turn(
            functools.partial(backward_kernel, last),
            (cotangent, from_next, w_first, w_second, unit, scale, slope),
            outs, rows, hidden, width, "last_backward_turn" if last else "backward_turn",
        )
        if not last:
            from_next = shifted(results[0], "code", -1)
    carried, slope_b, pre_slope = results

    late = lax.all_gather(
        jnp.concatenate([carried, slope_b], axis=1), "dp", axis=0, tiled=True
    )
    terms = temporal_terms(carried, gathered, n_dp, n_code, piece)
    terms = lax.all_to_all(terms, "code", 0, 0)
    temporal_grad = jnp.sum(terms.astype(F32), axis=0).astype(BF16)

    hidden_rows = jnp.concatenate(
        [active.reshape(n_dp, held, rows), pre_slope.reshape(n_dp, held, rows)], axis=1
    )
    hidden_rows = lax.all_to_all(hidden_rows, "dp", 0, 0)
    hidden_rows = hidden_rows.transpose(1, 0, 2).reshape(2 * held, n_dp * rows)
    active_all, pre_slope_all = hidden_rows[:held], hidden_rows[held:]
    first_grad = dot_nn(pre_slope_all, normed_all).astype(BF16)

    temporal_own = lax.dynamic_slice_in_dim(temporal_all, dp_index * piece, piece, 1).T
    own_vocab = table.shape[0] // n_dp
    vocab_ids = dp_index * own_vocab + lax.broadcasted_iota(jnp.int32, (own_vocab, 1), 0)
    onehot = (token_all[None, :] == vocab_ids).astype(BF16)
    left_carry = jnp.concatenate([temporal_own, onehot], axis=0)
    carry_grads, second_grad = final_grads(left_carry, active_all, late)
    return (
        temporal_grad,
        carry_grads[:piece][None],
        carry_grads[piece:][None],
        first_grad[:own_hidden].T[None],
        second_grad[:own_hidden].T[None],
    )


def solution(mesh):
    in_specs = (
        P("dp", None),
        P("code", "dp", None),
        P("code", None, None),
        P("code", None, "dp"),
        P("code", None, "dp"),
        P(None, "code"),
        P("dp"),
        P("dp", "code", None),
    )
    out_specs = (
        P("dp", "code"),
        P("code", "dp", None),
        P("code", "dp", None),
        P("code", None, "dp"),
        P("code", None, "dp"),
    )
    return jax.shard_map(
        per_device, mesh=mesh, in_specs=in_specs, out_specs=out_specs, check_vma=False
    )
```

time: 789 us -> 557 us (0.71)
  matrix products: 158 us -> 2.93 us
  blocking collectives: 140 us -> 0 us
  Pallas kernels: 0 us -> 80.6 us
  waiting for transfers between devices: 367 us -> 329 us
  starting transfers between devices: 47 us -> 80.7 us
  local copies, waits for them, and re-layouts: 53.7 us -> 32 us
    dot_general x23 -> x1, matrix products: 158 us -> 2.93 us  [dot_nn(): lax.dot_general(left, right, (((1,), (0,)), ((), ())), preferred_element_...]
    unnamed x1 -> x0, blocking collectives: 140 us -> none
    reduce_scatter x3 -> x0, waiting for transfers between devices: 104 us -> none  [the longest x1 76.9 us: per_device(): lax.psum_scatter(contract_rows(onehot, carried).astype(jnp.bfloat16), 'dp...]
    pallas_call x0 -> x19, Pallas kernels: none -> 80.6 us  [the longest x16 48.6 us: turn(): pl.pallas_call(kernel, in_specs=[VMEM] * len(operands), out_specs=jax.tre...]
    all_to_all x0 -> x2, starting transfers between devices: none -> 40.8 us  [the longest x1 24 us: per_device(): hidden_rows = lax.all_to_all(hidden_rows, 'dp', 0, 0)]
    all_to_all x0 -> x2, waiting for transfers between devices: none -> 40.8 us  [the longest x1 22 us: per_device(): hidden_rows = lax.all_to_all(hidden_rows, 'dp', 0, 0)]
    unnamed x26 -> x37, local copies, waits for them, and re-layouts: 50.6 us -> 12.5 us
    all_gather x3 -> x4, waiting for transfers between devices: 178 us -> 195 us  [the longest x1 115 us: per_device(): gathered = lax.all_gather(shard, 'dp', axis=0)]
  transfers between devices with their start and end apart: 22 -> 20, of which waited for: 20 -> 19; matrix products, arithmetic and copies ran while one was open for 27% -> 3% of each run, Pallas kernels for 0% -> 7%
where the time goes in v1:
time: 557 us; the launch traced here: 547 us
  waiting for transfers between devices  329 us (59%)
  starting transfers between devices  80.7 us (14%)
  Pallas kernels  80.6 us (14%)
  local copies, waits for them, and re-layouts  32 us (6%)
  between operations  14.6 us (3%)
  other arithmetic  7.46 us (1%)
    all_gather x1, waiting for transfers between devices, per_device(): gathered = lax.all_gather(shard, 'dp', axis=0)  115 us
    ppermute x14, waiting for transfers between devices, shifted(): return lax.ppermute(block, axis, route)  93.2 us
    all_gather x1, waiting for transfers between devices, per_device(): lax.all_gather(jnp.concatenate([carried, slope_b], axis=1), 'dp', axis=0,...  72.3 us
    pallas_call x16, Pallas kernels, turn(): pl.pallas_call(kernel, in_specs=[VMEM] * len(operands), out_specs=jax.tre...  48.6 us
    ppermute x14, starting transfers between devices, shifted(): return lax.ppermute(block, axis, route)  39.8 us
    all_to_all x1, starting transfers between devices, per_device(): hidden_rows = lax.all_to_all(hidden_rows, 'dp', 0, 0)  24 us
    all_to_all x1, waiting for transfers between devices, per_device(): hidden_rows = lax.all_to_all(hidden_rows, 'dp', 0, 0)  22 us
    all_to_all x1, waiting for transfers between devices, per_device(): terms = lax.all_to_all(terms, 'code', 0, 0)  18.7 us
  transfers between devices with their start and end apart: 20, of which 19 were waited for; matrix products, arithmetic and copies ran while one was open for 3% of the time, Pallas kernels for 7%

profile of v1, /device:TPU:1, one launch (start us, length us, event | category | flops | bytes accessed | tf_op | source)
XLA Modules:
  0.0 547.5 jit_solution(14672342529960907501)
XLA Ops:
  11.4 115.3 %all-gather.12.cloned.1.call-done = bf16[8448,1024]{1,0:T(8,128)(2,1)} async-done(((bf16[528,1024]{1,0:T(8,128)(2,1)}), bf16[8448,1024]{1,0:T(8,128)(2,1)}) %all-gather.12.cloned.1.call-update) | async-done | bytes 17301520 | tf_op jit(solution)/shard_map/all_gather | solution.py:230
  126.7 8.3 %fusion.9 = (bf16[16,136,1024]{2,1,0:T(8,128)(2,1)}, bf16[16,136,1024]{2,1,0:T(8,128)(2,1)}) fusion(bf16[16,528,1024]{2,1,0:T(8,128)(2,1)} %bitcast.84), kind=kLoop, calls=%fused_computation.31 | loop fusion | bytes 17825792 | tf_op jit(solution)/shard_map/slice | solution.py:232
  135.0 12.0 %depth_base.1.base_ref = f32[128,1024]{1,0:T(8,128)} custom-call(bf16[128,4096]{1,0:T(8,128)(2,1)} %t_ref.1, bf16[16,528,1024]{2,1,0:T(8,128)(2,1)} %bitcast.85, bf16[128,1024]{1,0:T(8,128)(2,1)} %broadcast_select_fusion.emb_ref), custom_call_target="tpu_custom_call" | custom-call | flops 1073741824 | bytes 8388608 | tf_op jit(solution)/shard_map/depth_base/pallas_call | solution.py:50
  155.8 3.2 collective-permute-start
  159.0 5.4 collective-permute-done.in_ref
  167.6 4.1 collective-permute-start.1
  171.7 4.5 collective-permute-done.1.in_ref
  179.4 4.1 collective-permute-start.2
  183.6 3.6 collective-permute-done.2.in_ref
  187.1 3.2 forward_turn.10
  190.3 4.3 collective-permute-start.3
  200.9 3.8 collective-permute-start.4
  204.8 3.3 collective-permute-done.4.in_ref
  211.3 4.3 collective-permute-start.5
  215.6 3.3 collective-permute-done.5.in_ref
  222.1 6.2 %collective-permute-start.6 = (bf16[128,1024]{1,0:T(8,128)(2,1)S(1)}, bf16[128,1024]{1,0:T(8,128)(2,1)S(1)}, u32[]{:S(2)}, u32[]{:S(2)}) collective-permute-start(bf16[128,1024]{1,0:T(8,128)(2,1)S(1)} %forward_turn.13), channel_id=1, source_target_pairs={{0,1},{1,2},{2,3},{3,4},{4,5},{5,6},{6,7},{8,9},{9,10},{10,11},{11... | collective-permute-start | bytes 786440 | tf_op jit(solution)/shard_map/ppermute | solution.py:27
  228.3 3.3 collective-permute-done.6.in_ref
  245.5 8.2 %collective-permute-done.7.next_ref = bf16[128,1024]{1,0:T(8,128)(2,1)S(1)} collective-permute-done((bf16[128,1024]{1,0:T(8,128)(2,1)S(1)}, bf16[128,1024]{1,0:T(8,128)(2,1)S(1)}, u32[]{:S(2)}, u32[]{:S(2)}) %collective-permute-start.7) | collective-permute-done | bytes 262176 | tf_op jit(solution)/shard_map/ppermute | solution.py:27
  260.2 8.9 %collective-permute-done.8.next_ref = bf16[128,1024]{1,0:T(8,128)(2,1)S(1)} collective-permute-done((bf16[128,1024]{1,0:T(8,128)(2,1)S(1)}, bf16[128,1024]{1,0:T(8,128)(2,1)S(1)}, u32[]{:S(2)}, u32[]{:S(2)}) %collective-permute-start.8) | collective-permute-done | bytes 262176 | tf_op jit(solution)/shard_map/ppermute | solution.py:27
  273.4 8.4 %collective-permute-done.9.next_ref = bf16[128,1024]{1,0:T(8,128)(2,1)S(1)} collective-permute-done((bf16[128,1024]{1,0:T(8,128)(2,1)S(1)}, bf16[128,1024]{1,0:T(8,128)(2,1)S(1)}, u32[]{:S(2)}, u32[]{:S(2)}) %collective-permute-start.9) | collective-permute-done | bytes 262176 | tf_op jit(solution)/shard_map/ppermute | solution.py:27
  286.1 11.4 %collective-permute-done.10.next_ref = bf16[128,1024]{1,0:T(8,128)(2,1)S(1)} collective-permute-done((bf16[128,1024]{1,0:T(8,128)(2,1)S(1)}, bf16[128,1024]{1,0:T(8,128)(2,1)S(1)}, u32[]{:S(2)}, u32[]{:S(2)}) %collective-permute-start.10) | collective-permute-done | bytes 262176 | tf_op jit(solution)/shard_map/ppermute | solution.py:27
  301.7 7.9 %collective-permute-done.11.next_ref = bf16[128,1024]{1,0:T(8,128)(2,1)S(1)} collective-permute-done((bf16[128,1024]{1,0:T(8,128)(2,1)S(1)}, bf16[128,1024]{1,0:T(8,128)(2,1)S(1)}, u32[]{:S(2)}, u32[]{:S(2)}) %collective-permute-start.11) | collective-permute-done | bytes 262176 | tf_op jit(solution)/shard_map/ppermute | solution.py:27
  314.4 13.7 %collective-permute-done.12.next_ref = bf16[128,1024]{1,0:T(8,128)(2,1)S(1)} collective-permute-done((bf16[128,1024]{1,0:T(8,128)(2,1)S(1)}, bf16[128,1024]{1,0:T(8,128)(2,1)S(1)}, u32[]{:S(2)}, u32[]{:S(2)}) %collective-permute-start.12) | collective-permute-done | bytes 262176 | tf_op jit(solution)/shard_map/ppermute | solution.py:27
  332.3 8.4 %collective-permute-done.13.next_ref = bf16[128,1024]{1,0:T(8,128)(2,1)S(1)} collective-permute-done((bf16[128,1024]{1,0:T(8,128)(2,1)S(1)}, bf16[128,1024]{1,0:T(8,128)(2,1)S(1)}, u32[]{:S(2)}, u32[]{:S(2)}) %collective-permute-start.13) | collective-permute-done | bytes 262176 | tf_op jit(solution)/shard_map/ppermute | solution.py:27
  344.6 12.9 %temporal_terms.1 = bf16[8,128,512]{2,1,0:T(8,128)(2,1)} custom-call(bf16[128,1024]{1,0:T(8,128)(2,1)} %copy-done.10, bf16[16,528,1024]{2,1,0:T(8,128)(2,1)} %bitcast.86), custom_call_target="tpu_custom_call" | custom-call | flops 1073741824 | bytes 8388608 | tf_op jit(solution)/shard_map/temporal_terms/pallas_call | solution.py:146
  357.5 16.8 %all-to-all-start = ((bf16[8,128,512]{2,1,0:T(8,128)(2,1)}), bf16[8,128,512]{2,1,0:T(8,128)(2,1)S(1)}, u32[]{:S(2)}, u32[]{:S(2)}) async-start(bf16[8,128,512]{2,1,0:T(8,128)(2,1)} %temporal_terms.1), calls=%async_computation | async-start | bytes 2097152 | tf_op jit(solution)/shard_map/all_to_all | solution.py:283
  375.5 18.7 %all-to-all-done = bf16[8,128,512]{2,1,0:T(8,128)(2,1)S(1)} async-done(((bf16[8,128,512]{2,1,0:T(8,128)(2,1)}), bf16[8,128,512]{2,1,0:T(8,128)(2,1)S(1)}, u32[]{:S(2)}, u32[]{:S(2)}) %all-to-all-start) | async-done | bytes 1048608 | tf_op jit(solution)/shard_map/all_to_all | solution.py:283
  394.2 24.0 %all-to-all-start.1 = ((bf16[16,272,128]{2,1,0:T(8,128)(2,1)}), bf16[16,272,128]{2,1,0:T(8,128)(2,1)S(1)}, u32[]{:S(2)}, u32[]{:S(2)}) async-start(bf16[16,272,128]{2,1,0:T(8,128)(2,1)} %pad_maximum_fusion.1), calls=%async_computation.1 | async-start | bytes 2228224 | tf_op jit(solution)/shard_map/all_to_all | solution.py:289
  419.1 22.0 %all-to-all-done.1 = bf16[16,272,128]{2,1,0:T(8,128)(2,1)S(1)} async-done(((bf16[16,272,128]{2,1,0:T(8,128)(2,1)}), bf16[16,272,128]{2,1,0:T(8,128)(2,1)S(1)}, u32[]{:S(2)}, u32[]{:S(2)}) %all-to-all-start.1) | async-done | bytes 1114144 | tf_op jit(solution)/shard_map/all_to_all | solution.py:289
  445.8 7.7 %all-gather.6.cloned.1.call-done = bf16[2048,4096]{0,1:T(8,128)(2,1)} async-done(((bf16[128,4096]{0,1:T(8,128)(2,1)}), bf16[2048,4096]{0,1:T(8,128)(2,1)}) %all-gather.6.cloned.1.call-update) | async-done | bytes 16777232 | tf_op jit(solution)/shard_map/all_gather | solution.py:238
  456.0 72.3 %all-gather.8.cloned.1.call-done.g_ref = bf16[2048,2048]{1,0:T(8,128)(2,1)} async-done(((bf16[128,2048]{1,0:T(8,128)(2,1)}), bf16[2048,2048]{1,0:T(8,128)(2,1)}) %all-gather.8.cloned.1.call-update) | async-done | bytes 8388624 | tf_op jit(solution)/shard_map/all_gather | solution.py:279
  528.3 7.1 %final_grads.1 = (bf16[320,1024]{1,0:T(8,128)(2,1)}, bf16[136,1024]{1,0:T(8,128)(2,1)}) custom-call(bf16[320,2048]{1,0:T(8,128)(2,1)} %pad_maximum_fusion.lc_ref, bf16[136,2048]{1,0:T(8,128)(2,1)} %bitcast.88, bf16[2048,2048]{1,0:T(8,128)(2,1)} %all-gather.8.cloned.1.call-done.g_ref), custom_call_target="tpu_custom_call" | custom-call | flops 1912602624 | bytes 8388608 | tf_op jit(solution)/shard_map/final_grads/pallas_call | solution.py:187
  (93 shorter events, 92.5 us)
Async XLA Ops:
  7.2 2.6 copy-start
  7.2 2.6 copy-start.12
  7.2 119.5 %all-gather.12.cloned.1.call-start = ((), (), s32[]{:S(2)}) async-start(), calls=%async_computation.5 | async-start | bytes 18382848 | tf_op jit(solution)/shard_map/all_gather | solution.py:230
  9.7 432.5 %all-gather.10.cloned.1.call-start = ((), (), s32[]{:S(2)}) async-start(), calls=%async_computation.4 | async-start | bytes 4456448 | tf_op jit(solution)/shard_map/all_gather | solution.py:261
  147.0 2.3 copy-start.2
  152.6 11.8 %copy-start.3 = (bf16[16,136,1024]{2,1,0:T(8,128)(2,1)S(1)}, bf16[16,136,1024]{2,1,0:T(8,128)(2,1)}, u32[]{:S(2)}) copy-start(bf16[16,136,1024]{2,1,0:T(8,128)(2,1)} %get-tuple-element.30) | copy-start | bytes 13369348
  152.6 11.8 %copy-start.6 = (bf16[16,136,1024]{2,1,0:T(8,128)(2,1)S(1)}, bf16[16,136,1024]{2,1,0:T(8,128)(2,1)}, u32[]{:S(2)}) copy-start(bf16[16,136,1024]{2,1,0:T(8,128)(2,1)} %get-tuple-element.29) | copy-start | bytes 13369348
  155.8 8.6 %collective-permute-start = (bf16[128,1024]{1,0:T(8,128)(2,1)S(1)}, bf16[128,1024]{1,0:T(8,128)(2,1)S(1)}, u32[]{:S(2)}, u32[]{:S(2)}) collective-permute-start(bf16[128,1024]{1,0:T(8,128)(2,1)S(1)} %forward_turn.7), channel_id=1, source_target_pairs={{0,1},{1,2},{2,3},{3,4},{4,5},{5,6},{6,7},{8,9},{9,10},{10,11},{11... | collective-permute-start | bytes 786440 | tf_op jit(solution)/shard_map/ppermute | solution.py:27
  167.6 8.6 %collective-permute-start.1 = (bf16[128,1024]{1,0:T(8,128)(2,1)S(1)}, bf16[128,1024]{1,0:T(8,128)(2,1)S(1)}, u32[]{:S(2)}, u32[]{:S(2)}) collective-permute-start(bf16[128,1024]{1,0:T(8,128)(2,1)S(1)} %forward_turn.8), channel_id=1, source_target_pairs={{0,1},{1,2},{2,3},{3,4},{4,5},{5,6},{6,7},{8,9},{9,10},{10,11},{11... | collective-permute-start | bytes 786440 | tf_op jit(solution)/shard_map/ppermute | solution.py:27
  179.4 7.7 %collective-permute-start.2 = (bf16[128,1024]{1,0:T(8,128)(2,1)S(1)}, bf16[128,1024]{1,0:T(8,128)(2,1)S(1)}, u32[]{:S(2)}, u32[]{:S(2)}) collective-permute-start(bf16[128,1024]{1,0:T(8,128)(2,1)S(1)} %forward_turn.9), channel_id=1, source_target_pairs={{0,1},{1,2},{2,3},{3,4},{4,5},{5,6},{6,7},{8,9},{9,10},{10,11},{11... | collective-permute-start | bytes 786440 | tf_op jit(solution)/shard_map/ppermute | solution.py:27
  190.3 7.4 %collective-permute-start.3 = (bf16[128,1024]{1,0:T(8,128)(2,1)S(1)}, bf16[128,1024]{1,0:T(8,128)(2,1)S(1)}, u32[]{:S(2)}, u32[]{:S(2)}) collective-permute-start(bf16[128,1024]{1,0:T(8,128)(2,1)S(1)} %forward_turn.10), channel_id=1, source_target_pairs={{0,1},{1,2},{2,3},{3,4},{4,5},{5,6},{6,7},{8,9},{9,10},{10,11},{11... | collective-permute-start | bytes 786440 | tf_op jit(solution)/shard_map/ppermute | solution.py:27
  200.9 7.1 %collective-permute-start.4 = (bf16[128,1024]{1,0:T(8,128)(2,1)S(1)}, bf16[128,1024]{1,0:T(8,128)(2,1)S(1)}, u32[]{:S(2)}, u32[]{:S(2)}) collective-permute-start(bf16[128,1024]{1,0:T(8,128)(2,1)S(1)} %forward_turn.11), channel_id=1, source_target_pairs={{0,1},{1,2},{2,3},{3,4},{4,5},{5,6},{6,7},{8,9},{9,10},{10,11},{11... | collective-permute-start | bytes 786440 | tf_op jit(solution)/shard_map/ppermute | solution.py:27
  211.3 7.6 %collective-permute-start.5 = (bf16[128,1024]{1,0:T(8,128)(2,1)S(1)}, bf16[128,1024]{1,0:T(8,128)(2,1)S(1)}, u32[]{:S(2)}, u32[]{:S(2)}) collective-permute-start(bf16[128,1024]{1,0:T(8,128)(2,1)S(1)} %forward_turn.12), channel_id=1, source_target_pairs={{0,1},{1,2},{2,3},{3,4},{4,5},{5,6},{6,7},{8,9},{9,10},{10,11},{11... | collective-permute-start | bytes 786440 | tf_op jit(solution)/shard_map/ppermute | solution.py:27
  222.1 9.5 %collective-permute-start.6 = (bf16[128,1024]{1,0:T(8,128)(2,1)S(1)}, bf16[128,1024]{1,0:T(8,128)(2,1)S(1)}, u32[]{:S(2)}, u32[]{:S(2)}) collective-permute-start(bf16[128,1024]{1,0:T(8,128)(2,1)S(1)} %forward_turn.13), channel_id=1, source_target_pairs={{0,1},{1,2},{2,3},{3,4},{4,5},{5,6},{6,7},{8,9},{9,10},{10,11},{11... | collective-permute-start | bytes 786440 | tf_op jit(solution)/shard_map/ppermute | solution.py:27
  233.9 2.5 copy-start.13
  233.9 2.5 copy-start.11
  233.9 219.6 %all-gather.6.cloned.1.call-start = ((), (), s32[]{:S(2)}) async-start(), calls=%async_computation.2 | async-start | bytes 17825792 | tf_op jit(solution)/shard_map/all_gather | solution.py:238
  236.2 17.4 %slice-start = ((s8[4456448]{0:T(1024)(128)(4,1)}), s8[262144]{0:T(1024)(128)(4,1)S(1)}, s32[]{:S(2)}) async-start(s8[4456448]{0:T(1024)(128)(4,1)} %bitcast.56), calls=%async_computation.6 | async-start | bytes 524288
  236.3 292.0 %all-gather.8.cloned.1.call-start = ((), (), s32[]{:S(2)}) async-start(), calls=%async_computation.3 | async-start | bytes 8912896 | tf_op jit(solution)/shard_map/all_gather | solution.py:279
  241.0 12.7 %slice-start.1 = ((s8[4456448]{0:T(1024)(128)(4,1)}), s8[4194304]{0:T(1024)(128)(4,1)S(1)}, s32[]{:S(2)}) async-start(s8[4456448]{0:T(1024)(128)(4,1)} %bitcast.56), calls=%async_computation.7 | async-start | bytes 8388608
  244.0 9.7 %collective-permute-start.7 = (bf16[128,1024]{1,0:T(8,128)(2,1)S(1)}, bf16[128,1024]{1,0:T(8,128)(2,1)S(1)}, u32[]{:S(2)}, u32[]{:S(2)}) collective-permute-start(bf16[128,1024]{1,0:T(8,128)(2,1)S(1)} %backward_turn.7), channel_id=1, source_target_pairs={{1,0},{2,1},{3,2},{4,3},{5,4},{6,5},{7,6},{9,8},{10,9},{11,10},{12... | collective-permute-start | bytes 786440 | tf_op jit(solution)/shard_map/ppermute | solution.py:27
  258.9 10.2 %collective-permute-start.8 = (bf16[128,1024]{1,0:T(8,128)(2,1)S(1)}, bf16[128,1024]{1,0:T(8,128)(2,1)S(1)}, u32[]{:S(2)}, u32[]{:S(2)}) collective-permute-start(bf16[128,1024]{1,0:T(8,128)(2,1)S(1)} %backward_turn.8), channel_id=1, source_target_pairs={{1,0},{2,1},{3,2},{4,3},{5,4},{6,5},{7,6},{9,8},{10,9},{11,10},{12... | collective-permute-start | bytes 786440 | tf_op jit(solution)/shard_map/ppermute | solution.py:27
  272.1 9.7 %collective-permute-start.9 = (bf16[128,1024]{1,0:T(8,128)(2,1)S(1)}, bf16[128,1024]{1,0:T(8,128)(2,1)S(1)}, u32[]{:S(2)}, u32[]{:S(2)}) collective-permute-start(bf16[128,1024]{1,0:T(8,128)(2,1)S(1)} %backward_turn.9), channel_id=1, source_target_pairs={{1,0},{2,1},{3,2},{4,3},{5,4},{6,5},{7,6},{9,8},{10,9},{11,10},{12... | collective-permute-start | bytes 786440 | tf_op jit(solution)/shard_map/ppermute | solution.py:27
  284.8 12.7 %collective-permute-start.10 = (bf16[128,1024]{1,0:T(8,128)(2,1)S(1)}, bf16[128,1024]{1,0:T(8,128)(2,1)S(1)}, u32[]{:S(2)}, u32[]{:S(2)}) collective-permute-start(bf16[128,1024]{1,0:T(8,128)(2,1)S(1)} %backward_turn.10), channel_id=1, source_target_pairs={{1,0},{2,1},{3,2},{4,3},{5,4},{6,5},{7,6},{9,8},{10,9},{11,10},{12... | collective-permute-start | bytes 786440 | tf_op jit(solution)/shard_map/ppermute | solution.py:27
  300.4 9.2 %collective-permute-start.11 = (bf16[128,1024]{1,0:T(8,128)(2,1)S(1)}, bf16[128,1024]{1,0:T(8,128)(2,1)S(1)}, u32[]{:S(2)}, u32[]{:S(2)}) collective-permute-start(bf16[128,1024]{1,0:T(8,128)(2,1)S(1)} %backward_turn.11), channel_id=1, source_target_pairs={{1,0},{2,1},{3,2},{4,3},{5,4},{6,5},{7,6},{9,8},{10,9},{11,10},{12... | collective-permute-start | bytes 786440 | tf_op jit(solution)/shard_map/ppermute | solution.py:27
  309.7 31.0 %slice-start.2 = ((s8[4456448]{0:T(1024)(128)(4,1)}), s8[4194304]{0:T(1024)(128)(4,1)S(1)}, s32[]{:S(2)}) async-start(s8[4456448]{0:T(1024)(128)(4,1)} %bitcast.79), calls=%async_computation.8 | async-start | bytes 8388608
  312.7 28.0 %slice-start.3 = ((s8[4456448]{0:T(1024)(128)(4,1)}), s8[262144]{0:T(1024)(128)(4,1)S(1)}, s32[]{:S(2)}) async-start(s8[4456448]{0:T(1024)(128)(4,1)} %bitcast.79), calls=%async_computation.9 | async-start | bytes 524288
  312.7 15.3 %collective-permute-start.12 = (bf16[128,1024]{1,0:T(8,128)(2,1)S(1)}, bf16[128,1024]{1,0:T(8,128)(2,1)S(1)}, u32[]{:S(2)}, u32[]{:S(2)}) collective-permute-start(bf16[128,1024]{1,0:T(8,128)(2,1)S(1)} %backward_turn.12), channel_id=1, source_target_pairs={{1,0},{2,1},{3,2},{4,3},{5,4},{6,5},{7,6},{9,8},{10,9},{11,10},{12... | collective-permute-start | bytes 786440 | tf_op jit(solution)/shard_map/ppermute | solution.py:27
  331.0 9.7 %collective-permute-start.13 = (bf16[128,1024]{1,0:T(8,128)(2,1)S(1)}, bf16[128,1024]{1,0:T(8,128)(2,1)S(1)}, u32[]{:S(2)}, u32[]{:S(2)}) collective-permute-start(bf16[128,1024]{1,0:T(8,128)(2,1)S(1)} %backward_turn.13), channel_id=1, source_target_pairs={{1,0},{2,1},{3,2},{4,3},{5,4},{6,5},{7,6},{9,8},{10,9},{11,10},{12... | collective-permute-start | bytes 786440 | tf_op jit(solution)/shard_map/ppermute | solution.py:27
  357.5 36.7 %all-to-all-start = ((bf16[8,128,512]{2,1,0:T(8,128)(2,1)}), bf16[8,128,512]{2,1,0:T(8,128)(2,1)S(1)}, u32[]{:S(2)}, u32[]{:S(2)}) async-start(bf16[8,128,512]{2,1,0:T(8,128)(2,1)} %temporal_terms.1), calls=%async_computation | async-start | bytes 2097152 | tf_op jit(solution)/shard_map/all_to_all | solution.py:283
  394.2 47.0 %all-to-all-start.1 = ((bf16[16,272,128]{2,1,0:T(8,128)(2,1)}), bf16[16,272,128]{2,1,0:T(8,128)(2,1)S(1)}, u32[]{:S(2)}, u32[]{:S(2)}) async-start(bf16[16,272,128]{2,1,0:T(8,128)(2,1)} %pad_maximum_fusion.1), calls=%async_computation.1 | async-start | bytes 2228224 | tf_op jit(solution)/shard_map/all_to_all | solution.py:289
  528.3 12.2 %copy-start.1 = (bf16[1,1024,1024]{2,1,0:T(8,128)(2,1)S(1)}, bf16[1,1024,1024]{2,1,0:T(8,128)(2,1)}, u32[]{:S(2)}) copy-start(bf16[1,1024,1024]{2,1,0:T(8,128)(2,1)} %param.10) | copy-start | bytes 6291460
  (6 other events, 11.0 us)
Sparse Core Ops, SparseCore 0:
  10.4 116.2 all-gather.11
  234.0 70.8 all-gather.9
  307.2 146.2 all-gather.5
  456.3 71.9 all-gather.7

commit v2 on v1

v2 whole, which is shorter than its diff:
```python
import functools

import jax
import jax.numpy as jnp
from jax import lax
from jax.experimental import pallas as pl
from jax.experimental.pallas import tpu as pltpu
from jax.sharding import PartitionSpec as P

EPS = 1e-06
F32 = jnp.float32
BF16 = jnp.bfloat16
SUBLANES = 8


def dot_nn(left, right):
    return lax.dot_general(left, right, (((1,), (0,)), ((), ())), preferred_element_type=F32)


def dot_nt(left, right):
    return lax.dot_general(left, right, (((1,), (1,)), ((), ())), preferred_element_type=F32)


def hop(block, axis, source, target):
    return lax.ppermute(block, axis, [(source, target)])


VMEM = pl.BlockSpec(memory_space=pltpu.VMEM)
ANY = pl.BlockSpec(memory_space=pl.ANY)


def params(megabytes):
    return pltpu.CompilerParams(vmem_limit_bytes=megabytes * 1024 * 1024)


def unpack_kernel(piece, held, t_ref, emb_ref, g_ref, after_ref, base_ref, w1_ref, w2_ref,
                  d_ref, d_sem, w_sem):
    n_dp = g_ref.shape[0]

    def depth_copy(s):
        return pltpu.make_async_copy(
            g_ref.at[s, pl.ds(0, piece)], d_ref.at[pl.ds(s * piece, piece)], d_sem.at[s]
        )

    def weight_copy(s, which):
        to_ref = (w1_ref, w2_ref)[which]
        return pltpu.make_async_copy(
            g_ref.at[s, pl.ds(piece + which * held, held)],
            to_ref.at[pl.ds(s * held, held)],
            w_sem.at[which, s],
        )

    for s in range(n_dp):
        depth_copy(s).start()
    for which in range(2):
        for s in range(n_dp):
            weight_copy(s, which).start()
    base_ref[...] = emb_ref[...].astype(F32)
    group = 4 if n_dp % 4 == 0 else 1
    span = group * piece

    def step(i, _):
        for j in range(group):
            depth_copy(i * group + j).wait()
        start = pl.multiple_of(i * span, span)
        base_ref[...] += dot_nn(t_ref[:, pl.ds(start, span)], d_ref[pl.ds(start, span), :])
        return 0

    lax.fori_loop(0, n_dp // group, step, 0)
    for which in range(2):
        for s in range(n_dp):
            weight_copy(s, which).wait()


def unpack(temporal, token_rows, gathered, after, piece, held):
    rows, _ = temporal.shape
    n_dp, _, width = gathered.shape
    hidden = n_dp * held
    weight = pltpu.VMEM((hidden, width), BF16)
    return pl.pallas_call(
        functools.partial(unpack_kernel, piece, held),
        in_specs=[VMEM, VMEM, pl.BlockSpec(memory_space=pltpu.HBM), ANY],
        out_specs=[VMEM] * 3,
        out_shape=[pltpu.VMEM((rows, width), F32), weight, weight],
        scratch_shapes=[
            pltpu.VMEM((n_dp * piece, width), BF16),
            pltpu.SemaphoreType.DMA((n_dp,)),
            pltpu.SemaphoreType.DMA((2, n_dp)),
        ],
        compiler_params=params(44),
        name="unpack",
    )(temporal, token_rows, gathered, after)


def chunks(hidden):
    return 4 if hidden % (4 * 2 * SUBLANES) == 0 else 1


def normalise(resid):
    scale = lax.rsqrt(jnp.mean(resid * resid, axis=-1, keepdims=True) + EPS)
    return scale, (resid * scale).astype(BF16)


def received(refs, start):
    for ref in refs:
        start = start + ref[...].astype(F32)
    return start


def hidden_loop(hidden, body, init):
    count = chunks(hidden)
    size = hidden // count
    return lax.fori_loop(
        0, count, lambda i, held: body(i, pl.ds(pl.multiple_of(i * size, size), size), held), init
    )


def forward_kernel(turn_index, code_ref, base_ref, w1_ref, w2_ref, *refs):
    out_ref = refs[-1]

    @pl.when(code_ref[0] == turn_index)
    def _():
        resid = received(refs[:-1], base_ref[...])
        _, normed = normalise(resid)

        def body(_, part, total):
            pre = dot_nt(normed, w1_ref[part, :])
            active = (pre * jax.nn.sigmoid(pre)).astype(BF16)
            return total + dot_nn(active, w2_ref[part, :])

        out_ref[...] = hidden_loop(w1_ref.shape[0], body, resid).astype(BF16)


def saved_kernel(base_ref, w1_ref, *refs):
    unit_ref, scale_ref, normed_ref, slope_ref, active_ref = refs[-5:]
    resid = received(refs[:-5], base_ref[...])
    scale, normed = normalise(resid)
    unit_ref[...] = resid * scale
    scale_ref[...] = scale
    normed_ref[...] = normed

    def body(i, part, _):
        pre = dot_nt(normed, w1_ref[part, :])
        sigma = jax.nn.sigmoid(pre)
        slope_ref[i] = sigma * (1.0 + pre * (1.0 - sigma))
        active_ref[part, :] = (pre * sigma).astype(BF16).T
        return 0

    hidden_loop(w1_ref.shape[0], body, 0)


def backward_math(state_slope, w1_ref, w2_ref, unit_ref, scale_ref, slope_ref, keep_ref):
    slope_b = state_slope.astype(BF16)

    def body(i, part, norm_slope):
        hidden = dot_nt(slope_b, w2_ref[part, :])
        pre_slope = (hidden * slope_ref[i]).astype(BF16)
        if keep_ref is not None:
            keep_ref[part, :] = pre_slope.T
        return norm_slope + dot_nn(pre_slope, w1_ref[part, :])

    norm_slope = hidden_loop(w1_ref.shape[0], body, jnp.zeros(state_slope.shape, F32))
    unit = unit_ref[...]
    mean = jnp.mean(norm_slope * unit, axis=-1, keepdims=True)
    carried = state_slope + scale_ref[...] * (norm_slope - unit * mean)
    return carried.astype(BF16), slope_b


def backward_kernel(
    owner, code_ref, cot_ref, w1_ref, w2_ref, unit_ref, scale_ref, slope_ref, *refs
):
    out_ref = refs[-1]

    @pl.when(code_ref[0] == owner)
    def _():
        state_slope = received(refs[:-1], cot_ref[...])
        out_ref[...], _ = backward_math(
            state_slope, w1_ref, w2_ref, unit_ref, scale_ref, slope_ref, None
        )


def last_kernel(cot_ref, w1_ref, w2_ref, unit_ref, scale_ref, slope_ref, *refs):
    late_ref, pre_ref = refs[-2:]
    width = cot_ref.shape[1]
    state_slope = received(refs[:-2], cot_ref[...])
    late_ref[:, :width], late_ref[:, width:] = backward_math(
        state_slope, w1_ref, w2_ref, unit_ref, scale_ref, slope_ref, pre_ref
    )


def turn(kernel, operands, outs, name, sizes):
    rows, hidden, width = sizes
    scalar = [pl.BlockSpec(memory_space=pltpu.SMEM)] if operands[0].dtype == jnp.int32 else []
    return pl.pallas_call(
        kernel,
        in_specs=scalar + [VMEM] * (len(operands) - len(scalar)),
        out_specs=jax.tree.map(lambda _: VMEM, outs),
        out_shape=outs,
        compiler_params=params(10),
        cost_estimate=pl.CostEstimate(
            flops=4 * rows * hidden * width, bytes_accessed=4 * hidden * width, transcendentals=0
        ),
        name=name,
    )(*operands)


def term_kernel(c_ref, w_ref, after_ref, out_ref):
    pieces, piece, width = w_ref.shape
    parts, _, columns = out_ref.shape
    terms = dot_nt(c_ref[...], w_ref[...].reshape(pieces * piece, width)).astype(BF16)
    for part in range(parts):
        out_ref[part] = terms[:, part * columns:(part + 1) * columns]


def temporal_terms(late, gathered, after, n_code, piece):
    rows = late.shape[0]
    n_dp, _, width = gathered.shape
    columns = n_dp * piece // n_code
    steps = 4 if n_dp % 4 == 0 and n_code % 4 == 0 else 1
    return pl.pallas_call(
        term_kernel,
        grid=(steps,),
        in_specs=[
            pl.BlockSpec((rows, width), lambda s: (0, 0)),
            pl.BlockSpec((n_dp // steps, piece, width), lambda s: (s, 0, 0)),
            ANY,
        ],
        out_specs=pl.BlockSpec((n_code // steps, rows, columns), lambda s: (s, 0, 0)),
        out_shape=jax.ShapeDtypeStruct((n_code, rows, columns), BF16),
        compiler_params=params(50),
        cost_estimate=pl.CostEstimate(
            flops=2 * rows * width * piece * n_dp,
            bytes_accessed=2 * width * piece * n_dp,
            transcendentals=0,
        ),
        name="temporal_terms",
    )(late, gathered, after)


def grads_kernel(lt_ref, lo_ref, ls_ref, g_ref, ot_ref, oo_ref, os_ref, at_ref, ao_ref, as_ref):
    step = pl.program_id(0)
    width = ot_ref.shape[1]
    work = ((lt_ref, ot_ref, at_ref, 0), (lo_ref, oo_ref, ao_ref, 0), (ls_ref, os_ref, as_ref, 1))

    @pl.when(step == 0)
    def _():
        for _, _, acc_ref, _ in work:
            acc_ref[...] = jnp.zeros_like(acc_ref)

    for left_ref, _, acc_ref, half in work:
        acc_ref[...] += dot_nn(left_ref[...], g_ref[:, half * width:(half + 1) * width])

    @pl.when(step == pl.num_programs(0) - 1)
    def _():
        for _, out_ref, acc_ref, _ in work:
            out_ref[...] = acc_ref[: out_ref.shape[0], :].astype(BF16)


def final_grads(lefts, out_rows, gathered):
    frames, both = gathered.shape
    width = both // 2
    block = 512 if frames % 512 == 0 else frames
    return pl.pallas_call(
        grads_kernel,
        grid=(frames // block,),
        in_specs=[pl.BlockSpec((left.shape[0], block), lambda s: (0, s)) for left in lefts]
        + [pl.BlockSpec((block, both), lambda s: (s, 0))],
        out_specs=[pl.BlockSpec((rows, width), lambda s: (0, 0)) for rows in out_rows],
        out_shape=[jax.ShapeDtypeStruct((rows, width), BF16) for rows in out_rows],
        scratch_shapes=[pltpu.VMEM((left.shape[0], width), F32) for left in lefts],
        compiler_params=params(58),
        cost_estimate=pl.CostEstimate(
            flops=2 * sum(left.shape[0] for left in lefts) * width * frames,
            bytes_accessed=2 * frames * both,
            transcendentals=0,
        ),
        name="final_grads",
    )(*lefts, gathered)


def per_device(
    temporal_out, depth_in, embed, depth_w1, depth_w2, audio_tokens, barge_mask, out_grad
):
    dp_index = lax.axis_index("dp")
    n_dp, n_code = lax.axis_size("dp"), lax.axis_size("code")
    rows = temporal_out.shape[0]
    piece, width = depth_in.shape[1:]
    own_hidden = depth_w1.shape[2]
    table = embed[0]

    pad_hidden = -own_hidden % SUBLANES
    held = own_hidden + pad_hidden
    hidden = held * n_dp
    pad = ((0, pad_hidden), (0, 0))
    shard = jnp.concatenate(
        [depth_in[0], jnp.pad(depth_w1[0].T, pad), jnp.pad(depth_w2[0].T, pad)], axis=0
    )
    gathered = lax.all_gather(shard, "dp", axis=0)
    token_all = audio_tokens[:, 0]
    token_own = lax.dynamic_slice_in_dim(token_all, dp_index * rows, rows, 0)
    token_rows = jnp.take(table, token_own, axis=0)
    temporal_all = lax.all_to_all(
        temporal_out.T.reshape(n_dp, piece, rows), "dp", 0, 0
    )
    base, w_first, w_second = unpack(
        temporal_out, token_rows, gathered, temporal_all, piece, held
    )

    code = lax.axis_index("code").astype(jnp.int32).reshape(1)
    sizes = (rows, hidden, width)
    state_type = jax.ShapeDtypeStruct((rows, width), BF16)
    got = []
    for step in range(n_code - 1):
        state = turn(
            functools.partial(forward_kernel, step),
            (code, base, w_first, w_second, *got[-1:]),
            state_type, "forward_turn", sizes,
        )
        got.append(hop(state, "code", step, step + 1))
    count = chunks(hidden)
    unit, scale, normed, slope, active = turn(
        saved_kernel,
        (base, w_first, *got),
        [
            jax.ShapeDtypeStruct((rows, width), F32),
            jax.ShapeDtypeStruct((rows, 1), F32),
            state_type,
            jax.ShapeDtypeStruct((count, rows, hidden // count), F32),
            jax.ShapeDtypeStruct((hidden, rows), BF16),
        ],
        "saved_values", sizes,
    )
    normed_all = lax.all_gather(normed, "dp", axis=0, tiled=True)

    cotangent = out_grad[:, 0, :].astype(F32) * barge_mask.astype(F32)[:, None]
    saved = (cotangent, w_first, w_second, unit, scale, slope)
    got = []
    for owner in range(n_code - 1, 0, -1):
        carried = turn(
            functools.partial(backward_kernel, owner), (code, *saved, *got[-1:]),
            state_type, "backward_turn", sizes,
        )
        got.append(hop(carried, "code", owner, owner - 1))
    late, pre_slope = turn(
        last_kernel, (*saved, *got),
        [
            jax.ShapeDtypeStruct((rows, 2 * width), BF16),
            jax.ShapeDtypeStruct((hidden, rows), BF16),
        ],
        "last_values", sizes,
    )

    late_all = lax.all_gather(late, "dp", axis=0, tiled=True)
    hidden_rows = jnp.concatenate(
        [active.reshape(n_dp, held, rows), pre_slope.reshape(n_dp, held, rows)], axis=1
    )
    hidden_rows = lax.all_to_all(hidden_rows, "dp", 0, 0)
    terms = temporal_terms(late, gathered, hidden_rows, n_code, piece)
    terms = lax.all_to_all(terms, "code", 0, 0)
    temporal_grad = jnp.sum(terms.astype(F32), axis=0).astype(BF16)

    hidden_rows = hidden_rows.transpose(1, 0, 2).reshape(2 * held, n_dp * rows)
    active_all, pre_slope_all = hidden_rows[:held], hidden_rows[held:]
    first_grad = dot_nn(pre_slope_all, normed_all).astype(BF16)

    temporal_own = temporal_all.transpose(1, 0, 2).reshape(piece, n_dp * rows)
    own_vocab = table.shape[0] // n_dp
    vocab_ids = dp_index * own_vocab + lax.broadcasted_iota(jnp.int32, (own_vocab, 1), 0)
    onehot = (token_all[None, :] == vocab_ids).astype(BF16)
    in_grad, table_grad, second_grad = final_grads(
        (temporal_own, onehot, active_all), (piece, own_vocab, own_hidden), late_all
    )
    return (
        temporal_grad,
        in_grad[None],
        table_grad[None],
        first_grad[:own_hidden].T[None],
        second_grad.T[None],
    )


def solution(mesh):
    in_specs = (
        P("dp", None),
        P("code", "dp", None),
        P("code", None, None),
        P("code", None, "dp"),
        P("code", None, "dp"),
        P(None, "code"),
        P("dp"),
        P("dp", "code", None),
    )
    out_specs = (
        P("dp", "code"),
        P("code", "dp", None),
        P("code", "dp", None),
        P("code", None, "dp"),
        P("code", None, "dp"),
    )
    return jax.shard_map(
        per_device, mesh=mesh, in_specs=in_specs, out_specs=out_specs, check_vma=False
    )
```

time: 557 us -> 417 us (0.75); the launches traced: 547 us -> 416 us
  Pallas kernels: 80.6 us -> 34.8 us
  starting transfers between devices: 80.7 us -> 36.5 us
  local copies, waits for them, and re-layouts: 32 us -> 9.71 us
  waiting for transfers between devices: 329 us -> 311 us
    all_gather x2 -> x1, waiting for transfers between devices: 79.9 us -> 17.7 us  [per_device(): late_all = lax.all_gather(late, 'dp', axis=0, tiled=True)]
    pallas_call x18, Pallas kernels: 73.5 us -> 27.3 us  [the longest x16 12.7 us: turn(): pl.pallas_call(kernel, in_specs=scalar + [VMEM] * (len(operands) - len(sc...]
    ppermute x14, waiting for transfers between devices: 93.2 us -> 137 us  [hop(): return lax.ppermute(block, axis, [(source, target)])]
    ppermute x14, starting transfers between devices: 39.8 us -> 11 us  [hop(): return lax.ppermute(block, axis, [(source, target)])]
    all_gather x1, waiting for transfers between devices: 115 us -> 92.9 us  [per_device(): gathered = lax.all_gather(shard, 'dp', axis=0)]
    all_to_all x0 -> x1, waiting for transfers between devices: none -> 19.9 us  [per_device(): lax.all_to_all(temporal_out.T.reshape(n_dp, piece, rows), 'dp', 0, 0)]
    all_to_all x1, starting transfers between devices: 16.8 us -> 4.38 us  [per_device(): terms = lax.all_to_all(terms, 'code', 0, 0)]
    all_to_all x1, starting transfers between devices: 24 us -> 12.5 us  [per_device(): hidden_rows = lax.all_to_all(hidden_rows, 'dp', 0, 0)]
  transfers between devices with their start and end apart: 20 -> 20, of which waited for: 19 -> 7; matrix products, arithmetic and copies ran while one was open for 3% -> 3% of each run, Pallas kernels for 7% -> 3%
where the time goes in v2:
time: 417 us; the launch traced here: 416 us
  waiting for transfers between devices  311 us (75%)
  starting transfers between devices  36.5 us (9%)
  Pallas kernels  34.8 us (8%)
  between operations  14.3 us (3%)
  local copies, waits for them, and re-layouts  9.71 us (2%)
  other arithmetic  6.72 us (2%)
    ppermute x14, waiting for transfers between devices, hop(): return lax.ppermute(block, axis, [(source, target)])  137 us
    all_gather x1, waiting for transfers between devices, per_device(): gathered = lax.all_gather(shard, 'dp', axis=0)  92.9 us
    all_to_all x1, waiting for transfers between devices, per_device(): hidden_rows = lax.all_to_all(hidden_rows, 'dp', 0, 0)  21.8 us
    all_to_all x1, waiting for transfers between devices, per_device(): terms = lax.all_to_all(terms, 'code', 0, 0)  21.4 us
    all_to_all x1, waiting for transfers between devices, per_device(): lax.all_to_all(temporal_out.T.reshape(n_dp, piece, rows), 'dp', 0, 0)  19.9 us
    all_gather x1, waiting for transfers between devices, per_device(): late_all = lax.all_gather(late, 'dp', axis=0, tiled=True)  17.7 us
    pallas_call x16, Pallas kernels, turn(): pl.pallas_call(kernel, in_specs=scalar + [VMEM] * (len(operands) - len(sc...  12.7 us
    all_to_all x1, starting transfers between devices, per_device(): hidden_rows = lax.all_to_all(hidden_rows, 'dp', 0, 0)  12.5 us
  transfers between devices with their start and end apart: 20, of which 7 were waited for; matrix products, arithmetic and copies ran while one was open for 3% of the time, Pallas kernels for 3%

profile of v2, /device:TPU:1, one launch (start us, length us, event | category | flops | bytes accessed | tf_op | source)
XLA Modules:
  0.0 416.0 jit_solution(6658357967660338056)
XLA Ops:
  7.2 2.5 fusion.4
  9.8 1.3 copy.16
  11.1 8.4 %all-to-all-start = ((bf16[16,256,128]{2,1,0:T(8,128)(2,1)}), bf16[16,256,128]{2,1,0:T(8,128)(2,1)S(1)}, u32[]{:S(2)}, u32[]{:S(2)}) async-start(bf16[16,256,128]{2,1,0:T(8,128)(2,1)} %bitcast.55), calls=%async_computation | async-start | bytes 2097152 | tf_op jit(solution)/shard_map/all_to_all | solution.py:302
  19.6 0.9 gather_fusion
  20.6 19.9 %all-to-all-done.after_ref = bf16[16,256,128]{2,1,0:T(8,128)(2,1)S(1)} async-done(((bf16[16,256,128]{2,1,0:T(8,128)(2,1)}), bf16[16,256,128]{2,1,0:T(8,128)(2,1)S(1)}, u32[]{:S(2)}, u32[]{:S(2)}) %all-to-all-start) | async-done | bytes 1048608 | tf_op jit(solution)/shard_map/all_to_all | solution.py:302
  40.5 92.9 %all-gather.9.cloned.1.call-done = bf16[8448,1024]{1,0:T(8,128)(2,1)} async-done(((bf16[528,1024]{1,0:T(8,128)(2,1)}), bf16[8448,1024]{1,0:T(8,128)(2,1)}) %all-gather.9.cloned.1.call-update) | async-done | bytes 17301520 | tf_op jit(solution)/shard_map/all_gather | solution.py:298
  133.4 8.0 %unpack.1 = (f32[128,1024]{1,0:T(8,128)S(1)}, bf16[2176,1024]{1,0:T(8,128)(2,1)S(1)}, bf16[2176,1024]{1,0:T(8,128)(2,1)S(1)}) custom-call(bf16[128,4096]{1,0:T(8,128)(2,1)} %t_ref.1, bf16[128,1024]{1,0:T(8,128)(2,1)S(1)} %broadcast_select_fusion.emb_ref, bf16[16,528,1024]{2,1,0:T(8,128)(2,1)} %bitcast.52, bf16[16,256,128]{2,1,0:T(8,128)(2,1)} %copy-done.6), custom_call_target="tpu_custom_call" | custom-call | tf_op jit(solution)/shard_map/unpack/pallas_call | solution.py:80
  141.4 4.2 %forward_turn.7 = bf16[128,1024]{1,0:T(8,128)(2,1)S(1)} custom-call(s32[1]{0:T(128)} %bitcast.12.code_ref, f32[128,1024]{1,0:T(8,128)S(1)} %get-tuple-element.20.base_ref, bf16[2176,1024]{1,0:T(8,128)(2,1)S(1)} %get-tuple-element.18.w1_ref, bf16[2176,1024]{1,0:T(8,128)(2,1)S(1)} %get-tuple-element.19.w2_ref), custom_call_target="tpu_custom_call" | custom-call | flops 1140850688 | bytes 8912896 | tf_op jit(solution)/shard_map/forward_turn/pallas_call | solution.py:194
  145.6 1.3 collective-permute-start
  146.9 5.7 %collective-permute-done.refs_0_ = bf16[128,1024]{1,0:T(8,128)(2,1)S(1)} collective-permute-done((bf16[128,1024]{1,0:T(8,128)(2,1)S(1)}, bf16[128,1024]{1,0:T(8,128)(2,1)S(1)}, u32[]{:S(2)}, u32[]{:S(2)}) %collective-permute-start) | collective-permute-done | bytes 262176 | tf_op jit(solution)/shard_map/ppermute | solution.py:25
  156.2 0.8 collective-permute-start.6
  157.1 3.0 saved_values.1
  160.3 2.3 copy-done.3
  162.5 2.3 copy-done.5
  166.2 0.9 collective-permute-start.9
  169.2 1.3 collective-permute-start.13
  170.5 131.7 %collective-permute-done.13.refs_6_ = bf16[128,1024]{1,0:T(8,128)(2,1)S(1)} collective-permute-done((bf16[128,1024]{1,0:T(8,128)(2,1)S(1)}, bf16[128,1024]{1,0:T(8,128)(2,1)S(1)}, u32[]{:S(2)}, u32[]{:S(2)}) %collective-permute-start.13) | collective-permute-done | bytes 262176 | tf_op jit(solution)/shard_map/ppermute | solution.py:25
  302.2 5.4 %last_values.1 = (bf16[128,2048]{1,0:T(8,128)(2,1)}, bf16[2176,128]{1,0:T(8,128)(2,1)S(1)}) custom-call(f32[128,1024]{1,0:T(8,128)S(1)} %convert_multiply_fusion.cot_ref, bf16[2176,1024]{1,0:T(8,128)(2,1)S(1)} %copy-done.3, bf16[2176,1024]{1,0:T(8,128)(2,1)S(1)} %copy-done.5, f32[128,1024]{1,0:T(8,128)S(1)} %get-tuple-element.21.unit_ref, ...), custom_call_target="tpu_custom_call" | custom-call | flops 1140850688 | bytes 8912896 | tf_op jit(solution)/shard_map/last_values/pallas_call | solution.py:194
  307.6 1.1 pad_maximum_fusion
  308.7 12.5 %all-to-all-start.1 = ((bf16[16,272,128]{2,1,0:T(8,128)(2,1)}), bf16[16,272,128]{2,1,0:T(8,128)(2,1)S(1)}, u32[]{:S(2)}, u32[]{:S(2)}) async-start(bf16[16,272,128]{2,1,0:T(8,128)(2,1)} %pad_maximum_fusion), calls=%async_computation.1 | async-start | bytes 2228224 | tf_op jit(solution)/shard_map/all_to_all | solution.py:357
  321.3 21.8 %all-to-all-done.1.after_ref = bf16[16,272,128]{2,1,0:T(8,128)(2,1)S(1)} async-done(((bf16[16,272,128]{2,1,0:T(8,128)(2,1)}), bf16[16,272,128]{2,1,0:T(8,128)(2,1)S(1)}, u32[]{:S(2)}, u32[]{:S(2)}) %all-to-all-start.1) | async-done | bytes 1114144 | tf_op jit(solution)/shard_map/all_to_all | solution.py:357
  343.1 6.7 %temporal_terms.1 = bf16[8,128,512]{2,1,0:T(8,128)(2,1)} custom-call(bf16[128,2048]{1,0:T(8,128)(2,1)} %get-tuple-element.24.c_ref, bf16[16,528,1024]{2,1,0:T(8,128)(2,1)} %bitcast.53, bf16[16,272,128]{2,1,0:T(8,128)(2,1)S(1)} %all-to-all-done.1.after_ref), custom_call_target="tpu_custom_call" | custom-call | flops 1073741824 | bytes 8388608 | tf_op jit(solution)/shard_map/temporal_terms/pallas_call | solution.py:220
  349.7 4.4 %all-to-all-start.2 = ((bf16[8,128,512]{2,1,0:T(8,128)(2,1)}), bf16[8,128,512]{2,1,0:T(8,128)(2,1)}, u32[]{:S(2)}, u32[]{:S(2)}) async-start(bf16[8,128,512]{2,1,0:T(8,128)(2,1)} %temporal_terms.1), calls=%async_computation.2 | async-start | bytes 2097152 | tf_op jit(solution)/shard_map/all_to_all | solution.py:359
  354.1 0.8 compare_convert_fusion.lo_ref
  355.0 1.2 copy_bitcast_fusion.lt_ref
  356.2 1.0 copy.29
  357.2 21.4 %all-to-all-done.2 = bf16[8,128,512]{2,1,0:T(8,128)(2,1)} async-done(((bf16[8,128,512]{2,1,0:T(8,128)(2,1)}), bf16[8,128,512]{2,1,0:T(8,128)(2,1)}, u32[]{:S(2)}, u32[]{:S(2)}) %all-to-all-start.2) | async-done | bytes 1048608 | tf_op jit(solution)/shard_map/all_to_all | solution.py:359
  378.6 2.1 reduce_sum.12
  380.7 2.9 fusion.5
  383.6 0.7 fusion.8
  384.4 17.7 %all-gather.5.cloned.1.call-done.g_ref = bf16[2048,2048]{1,0:T(8,128)(2,1)} async-done(((bf16[128,2048]{1,0:T(8,128)(2,1)}), bf16[2048,2048]{1,0:T(8,128)(2,1)}) %all-gather.5.cloned.1.call-update) | async-done | bytes 8388624 | tf_op jit(solution)/shard_map/all_gather | solution.py:353
  402.1 7.4 %final_grads.1 = (bf16[256,1024]{1,0:T(8,128)(2,1)}, bf16[64,1024]{1,0:T(8,128)(2,1)}, bf16[132,1024]{1,0:T(8,128)(2,1)}) custom-call(bf16[256,2048]{1,0:T(8,128)(2,1)} %copy_bitcast_fusion.lt_ref, bf16[64,2048]{1,0:T(8,128)(2,1)} %compare_convert_fusion.lo_ref, bf16[136,2048]{1,0:T(8,128)(2,1)} %bitcast.56, ...), custom_call_target="tpu_custom_call" | custom-call | flops 1912602624 | bytes 8388608 | tf_op jit(solution)/shard_map/final_grads/pallas_call | solution.py:263
  (71 shorter events, 7.4 us)
Async XLA Ops:
  7.2 12.5 %copy-start = (bf16[1,1024,1024]{2,1,0:T(8,128)(2,1)S(1)}, bf16[1,1024,1024]{2,1,0:T(8,128)(2,1)}, u32[]{:S(2)}) copy-start(bf16[1,1024,1024]{2,1,0:T(8,128)(2,1)} %param.10) | copy-start | bytes 6291460
  7.2 2.6 copy-start.8
  7.2 126.2 %all-gather.9.cloned.1.call-start = ((), (), s32[]{:S(2)}) async-start(), calls=%async_computation.5 | async-start | bytes 18382848 | tf_op jit(solution)/shard_map/all_gather | solution.py:298
  9.8 9.8 %copy-start.10 = (s32[2048,1]{0,1:T(1,128)S(1)}, s32[2048,1]{0,1:T(1,128)}, u32[]{:S(2)}) copy-start(s32[2048,1]{0,1:T(1,128)} %param.13) | copy-start | bytes 24580
  11.1 29.4 %all-to-all-start = ((bf16[16,256,128]{2,1,0:T(8,128)(2,1)}), bf16[16,256,128]{2,1,0:T(8,128)(2,1)S(1)}, u32[]{:S(2)}, u32[]{:S(2)}) async-start(bf16[16,256,128]{2,1,0:T(8,128)(2,1)} %bitcast.55), calls=%async_computation | async-start | bytes 2097152 | tf_op jit(solution)/shard_map/all_to_all | solution.py:302
  19.5 361.1 %all-gather.7.cloned.1.call-start = ((), (), s32[]{:S(2)}) async-start(), calls=%async_computation.4 | async-start | bytes 4456448 | tf_op jit(solution)/shard_map/all_gather | solution.py:333
  40.5 92.9 %copy-start.6 = (bf16[16,256,128]{2,1,0:T(8,128)(2,1)}, bf16[16,256,128]{2,1,0:T(8,128)(2,1)S(1)}, u32[]{:S(2)}) copy-start(bf16[16,256,128]{2,1,0:T(8,128)(2,1)S(1)} %all-to-all-done.after_ref) | copy-start | bytes 3145732
  141.4 14.8 %copy-start.4 = (bf16[2176,1024]{1,0:T(8,128)(2,1)}, bf16[2176,1024]{1,0:T(8,128)(2,1)S(1)}, u32[]{:S(2)}) copy-start(bf16[2176,1024]{1,0:T(8,128)(2,1)S(1)} %get-tuple-element.19.w2_ref) | copy-start | bytes 13369348
  141.4 15.7 %copy-start.2 = (bf16[2176,1024]{1,0:T(8,128)(2,1)}, bf16[2176,1024]{1,0:T(8,128)(2,1)S(1)}, u32[]{:S(2)}) copy-start(bf16[2176,1024]{1,0:T(8,128)(2,1)S(1)} %get-tuple-element.18.w1_ref) | copy-start | bytes 13369348
  145.6 7.1 %collective-permute-start = (bf16[128,1024]{1,0:T(8,128)(2,1)S(1)}, bf16[128,1024]{1,0:T(8,128)(2,1)S(1)}, u32[]{:S(2)}, u32[]{:S(2)}) collective-permute-start(bf16[128,1024]{1,0:T(8,128)(2,1)S(1)} %forward_turn.7), channel_id=1, source_target_pairs={{0,1},{8,9},{16,17},{24,25},{32,33},{40,41},{48,49},{56,57},{64,65... | collective-permute-start | bytes 786440 | tf_op jit(solution)/shard_map/ppermute | solution.py:25
  152.6 0.7 collective-permute-start.1
  153.3 0.7 collective-permute-start.2
  154.1 0.7 collective-permute-start.3
  154.8 0.7 collective-permute-start.4
  155.5 0.7 collective-permute-start.5
  156.2 3.9 copy-start.11
  156.2 3.9 copy-start.9
  156.2 0.8 collective-permute-start.6
  160.1 242.0 %all-gather.5.cloned.1.call-start = ((), (), s32[]{:S(2)}) async-start(), calls=%async_computation.3 | async-start | bytes 8912896 | tf_op jit(solution)/shard_map/all_gather | solution.py:353
  160.3 2.3 copy-start.3
  162.5 2.3 copy-start.5
  164.8 0.7 collective-permute-start.7
  165.5 0.7 collective-permute-start.8
  166.2 0.9 collective-permute-start.9
  167.1 0.7 collective-permute-start.10
  167.8 0.7 collective-permute-start.11
  168.5 0.7 collective-permute-start.12
  169.2 133.0 %collective-permute-start.13 = (bf16[128,1024]{1,0:T(8,128)(2,1)S(1)}, bf16[128,1024]{1,0:T(8,128)(2,1)S(1)}, u32[]{:S(2)}, u32[]{:S(2)}) collective-permute-start(bf16[128,1024]{1,0:T(8,128)(2,1)S(1)} %backward_turn.13), channel_id=1, source_target_pairs={{1,0},{9,8},{17,16},{25,24},{33,32},{41,40},{49,48},{57,56},{65,64... | collective-permute-start | bytes 786440 | tf_op jit(solution)/shard_map/ppermute | solution.py:25
  308.7 34.3 %all-to-all-start.1 = ((bf16[16,272,128]{2,1,0:T(8,128)(2,1)}), bf16[16,272,128]{2,1,0:T(8,128)(2,1)S(1)}, u32[]{:S(2)}, u32[]{:S(2)}) async-start(bf16[16,272,128]{2,1,0:T(8,128)(2,1)} %pad_maximum_fusion), calls=%async_computation.1 | async-start | bytes 2228224 | tf_op jit(solution)/shard_map/all_to_all | solution.py:357
  349.7 5.2 %copy-start.7 = (bf16[16,256,128]{2,1,0:T(8,128)(2,1)S(1)}, bf16[16,256,128]{2,1,0:T(8,128)(2,1)}, u32[]{:S(2)}) copy-start(bf16[16,256,128]{2,1,0:T(8,128)(2,1)} %copy-done.6) | copy-start | bytes 3145732
  349.7 28.9 %all-to-all-start.2 = ((bf16[8,128,512]{2,1,0:T(8,128)(2,1)}), bf16[8,128,512]{2,1,0:T(8,128)(2,1)}, u32[]{:S(2)}, u32[]{:S(2)}) async-start(bf16[8,128,512]{2,1,0:T(8,128)(2,1)} %temporal_terms.1), calls=%async_computation.2 | async-start | bytes 2097152 | tf_op jit(solution)/shard_map/all_to_all | solution.py:359
  402.1 7.4 %copy-start.1 = (bf16[1,1024,1024]{2,1,0:T(8,128)(2,1)S(1)}, bf16[1,1024,1024]{2,1,0:T(8,128)(2,1)}, u32[]{:S(2)}) copy-start(bf16[1,1024,1024]{2,1,0:T(8,128)(2,1)} %param.10) | copy-start | bytes 6291460
Sparse Core Ops, SparseCore 0:
  10.4 122.9 all-gather.8
  160.2 119.6 all-gather.6
  307.8 94.2 all-gather.4
